TPU v7x, 128 devices: a whole 4x4x4 slice. The times are simulated.
128 devices in a mesh: seq: 16 (over z, y_lo, core), grp: 8 (over y_hi, x).
Axes of the slice: x: 4, y: 4 (y_hi: 2, y_lo: 2; y = y_hi * 2 + y_lo), z: 4, core: 2. Of those that a mesh axis runs over, the one named last changes fastest.
Arguments:
- layer_input: bfloat16 [8, 8192, 4096], P('grp', 'seq'), may hold values from -6 to 6
- queries: bfloat16 [8, 8192, 2048], P('grp', 'seq'), may hold values from -6 to 6
- key_vectors: bfloat16 [8, 8192, 2048], P('grp', 'seq'), may hold values from -6 to 6
- value_vectors: bfloat16 [8, 8192, 2048], P('grp', 'seq'), may hold values from -6 to 6
- grad_output: bfloat16 [8, 8192, 2048], P('grp', 'seq'), may hold values from -0.015625 to 0.015625
Outputs:
- grad_queries: bfloat16 [8, 8192, 2048], P('grp', 'seq')
- grad_keys: bfloat16 [8, 8192, 2048], P('grp', 'seq')
- grad_values: bfloat16 [8, 8192, 2048], P('grp', 'seq')
- grad_weight: float32 [4096, 2048], P('seq', 'grp')
All inputs are finite; a program needn't handle non-finite values.
Results may differ from a plain program's by a relative error of at most 0.0049.
Values sent between devices are 32-bit elements; how exact they have to be, the bound alone decides.
A program may use at most 192 MiB of HBM per device.

v0:
```python
import jax
import jax.numpy as jnp
from jax import lax
from jax.sharding import PartitionSpec as P

H = 16
HDIM = 128
BLK = 512
HD = 2048


def prefix(value, axis, join, neutral, backward):
    count, mine = (lax.axis_size(axis), lax.axis_index(axis))
    pieces = lax.all_gather(value, axis)
    if backward:
        pieces = pieces[::-1]
        mine = count - 1 - mine
    total = jnp.full_like(value, 0) + jnp.asarray(neutral, value.dtype)

    def step(position, total):
        longer = join(total, pieces[position])
        return jnp.where(position < mine, longer, total)

    return lax.fori_loop(0, count - 1, step, total)


def add_states(earlier, later):
    return earlier + later


def per_device(layer_input, queries, key_vectors, value_vectors, grad_output):
    tok_rows = queries.shape[1]
    block_len = min(tok_rows, BLK)
    block_count = tok_rows // block_len

    def split(array):
        return array.reshape(block_count, block_len, H, HDIM)

    q_blocks = split(queries)
    k_blocks = split(key_vectors)
    v_blocks = split(value_vectors)
    g_blocks = split(grad_output)
    kv_sum = jnp.einsum("bthe,bthf->bhef", k_blocks, v_blocks, preferred_element_type=jnp.float32)
    qg_sum = jnp.einsum("bthe,bthf->bhef", q_blocks, g_blocks, preferred_element_type=jnp.float32)
    kv_device = jnp.sum(kv_sum, axis=0)
    qg_device = jnp.sum(qg_sum, axis=0)
    zero_state = jnp.zeros((H, HDIM, HDIM), jnp.float32)
    before_device = prefix(kv_device, "seq", add_states, zero_state, False)
    after_device = prefix(qg_device, "seq", add_states, zero_state, True)
    before = before_device + (jnp.cumsum(kv_sum, axis=0) - kv_sum)
    after = after_device + (qg_device - jnp.cumsum(qg_sum, axis=0))
    before_r = before.astype(jnp.bfloat16)
    after_r = after.astype(jnp.bfloat16)
    causal = jnp.tril(jnp.ones((block_len, block_len), dtype=bool))
    within = jnp.where(
        causal,
        jnp.einsum("bthe,bshe->bhts", q_blocks, k_blocks, preferred_element_type=jnp.float32),
        0.0,
    ).astype(jnp.bfloat16)
    back = jnp.where(
        causal,
        jnp.einsum("bthf,bshf->bhts", g_blocks, v_blocks, preferred_element_type=jnp.float32),
        0.0,
    ).astype(jnp.bfloat16)
    grad_q = jnp.einsum(
        "bhts,bshe->bthe", back, k_blocks, preferred_element_type=jnp.float32
    ) + jnp.einsum("bthf,bhef->bthe", g_blocks, before_r, preferred_element_type=jnp.float32)
    grad_k = jnp.einsum(
        "bhts,bthe->bshe", back, q_blocks, preferred_element_type=jnp.float32
    ) + jnp.einsum("bshf,bhef->bshe", v_blocks, after_r, preferred_element_type=jnp.float32)
    grad_v = jnp.einsum(
        "bhts,bthf->bshf", within, g_blocks, preferred_element_type=jnp.float32
    ) + jnp.einsum("bshe,bhef->bshf", k_blocks, after_r, preferred_element_type=jnp.float32)
    grad_queries = grad_q.astype(jnp.bfloat16).reshape(1, tok_rows, HD)
    grad_keys = grad_k.astype(jnp.bfloat16).reshape(1, tok_rows, HD)
    grad_values = grad_v.astype(jnp.bfloat16).reshape(1, tok_rows, HD)
    input_rows = layer_input[0]
    value_rows = grad_values[0]
    seq_total = lax.psum_scatter(
        lax.dot_general(
            input_rows, value_rows, (((0,), (0,)), ((), ())), preferred_element_type=jnp.float32
        ),
        "seq",
        scatter_dimension=0,
        tiled=True,
    )
    weight_share = lax.psum_scatter(seq_total, "grp", scatter_dimension=1, tiled=True)
    token_total = tok_rows * lax.axis_size("seq") * lax.axis_size("grp")
    grad_weight = weight_share * float(token_total) ** (-0.5)
    return (grad_queries, grad_keys, grad_values, grad_weight)


def solution(mesh):
    return jax.shard_map(
        per_device,
        mesh=mesh,
        in_specs=(
            P("grp", "seq", None),
            P("grp", "seq", None),
            P("grp", "seq", None),
            P("grp", "seq", None),
            P("grp", "seq", None),
        ),
        out_specs=(
            P("grp", "seq", None),
            P("grp", "seq", None),
            P("grp", "seq", None),
            P("seq", "grp"),
        ),
        check_vma=False,
    )
```

profile of v0, /device:TPU:0, one launch (start us, length us, event | category | flops | bytes accessed | tf_op | source)
XLA Modules:
  0.0 700.3 jit_solution(3804564928399747514)
XLA Ops:
  7.2 2.9 copy.45
  10.1 2.2 copy.48
  13.7 2.2 fusion.5
  16.0 3.5 copy.47
  19.6 8.1 %fusion.4 = f32[16,512,128]{1,2,0:T(8,128)} fusion(bf16[512,16,128]{0,2,1:T(8,128)(2,1)S(1)} %bitcast.64, pred[512,512]{1,0:T(8,128)(4,1)S(1)} %iota_compare_fusion, bf16[512,16,128]{2,1,0:T(8,128)(2,1)} %bitcast.72, bf16[512,16,128]{2,1,0:T(8,128)(2,1)} %bitcast.67), kind=kOutput, calls=%fused_computation.12 | convolution fusion | flops 2155872256 | bytes 10747904 | tf_op jit(solution)/shard_map/bhts,bthf->bshf/dot_general | solution.py:71
  27.7 82.5 %all-gather.7.cloned.1.call-done = f32[256,128,128]{2,1,0:T(8,128)} async-done(((f32[16,128,128]{2,1,0:T(8,128)}), f32[256,128,128]{2,1,0:T(8,128)}) %all-gather.7.cloned.1.call-update) | async-done | bytes 16777232 | tf_op jit(solution)/shard_map/all_gather | solution.py:14
  110.2 11.6 %rev.3 = f32[16,16,128,128]{3,2,1,0:T(8,128)} reverse(f32[16,16,128,128]{3,2,1,0:T(8,128)} %bitcast.74), dimensions={0} | reverse | bytes 33554432 | tf_op jit(solution)/shard_map/rev | solution.py:16
  121.9 24.2 %while.29 = (s32[]{:T(128)}, f32[16,128,128]{2,1,0:T(8,128)S(1)}, s32[]{:T(128)}, f32[16,16,128,128]{3,2,1,0:T(8,128)}, s32[]{:T(128)}, /*index=5*/s32[]{:T(128)}) while((s32[]{:T(128)}, f32[16,128,128]{2,1,0:T(8,128)S(1)}, s32[]{:T(128)}, f32[16,16,128,128]{3,2,1,0:T(8,128)}, s32[]{:T(128)}, /*index=5*/s32[]{:T(128)}) %tuple.68), condition=%wide.region_3.4_spmd.clone, body=%wide.region_2.3_spmd.clone.sunk | while | flops 786436 | bytes 3145821 | solution.py:24
  125.1 1.6 add_select_fusion.5
  128.3 1.6 add_select_fusion.5
  131.6 1.6 add_select_fusion.5
  133.2 1.6 add_select_fusion.5
  134.8 1.6 add_select_fusion.5
  148.0 3.9 fusion.1
  153.2 14.5 %convolution_bitcast_fusion = f32[4096,2048]{0,1:T(8,128)} fusion(bf16[512,2048]{0,1:T(8,128)(2,1)S(1)} %bitcast.75, bf16[1,512,4096]{2,1,0:T(8,128)(2,1)S(1)} %copy-done.9), kind=kOutput, calls=%fused_computation.2 | convolution fusion | flops 8589934592 | bytes 39845888 | tf_op jit(solution)/shard_map/dot_general | solution.py:80
  168.0 2.4 copy.46
  171.7 2.9 fusion.12
  174.7 7.7 %select_convert_fusion.1 = bf16[16,512,512]{2,1,0:T(8,128)(2,1)} fusion(bf16[512,16,128]{0,2,1:T(8,128)(2,1)S(1)} %bitcast.65, pred[512,512]{1,0:T(8,128)(4,1)S(1)} %iota_compare_fusion, bf16[512,16,128]{2,1,0:T(8,128)(2,1)} %bitcast.78), kind=kOutput, calls=%fused_computation.4 | convolution fusion | flops 1082130432 | bytes 12845056 | tf_op jit(solution)/shard_map/bthf,bshf->bhts/dot_general | solution.py:62
  182.4 337.5 %reduce-scatter.3.cloned.1.call-done = f32[256,2048]{0,1:T(8,128)} async-done(((f32[4096,2048]{0,1:T(8,128)}), f32[256,2048]{0,1:T(8,128)}) %reduce-scatter.3.cloned.1.call-update) | async-done | bytes 2097168 | tf_op jit(solution)/shard_map/reduce_scatter | solution.py:79
  519.9 92.0 %all-gather.5.cloned.1.call-done = f32[256,128,128]{2,1,0:T(8,128)} async-done(((f32[16,128,128]{2,1,0:T(8,128)}), f32[256,128,128]{2,1,0:T(8,128)}) %all-gather.5.cloned.1.call-update) | async-done | bytes 16777232 | tf_op jit(solution)/shard_map/all_gather | solution.py:14
  611.9 24.3 %while.28 = (s32[]{:T(128)}, f32[16,128,128]{2,1,0:T(8,128)S(1)}, s32[]{:T(128)}, f32[16,16,128,128]{3,2,1,0:T(8,128)}, s32[]{:T(128)}, /*index=5*/s32[]{:T(128)}) while((s32[]{:T(128)}, f32[16,128,128]{2,1,0:T(8,128)S(1)}, s32[]{:T(128)}, f32[16,16,128,128]{3,2,1,0:T(8,128)}, s32[]{:T(128)}, /*index=5*/s32[]{:T(128)}) %tuple.79), condition=%wide.region_1.0_spmd.clone, body=%wide.region_0.0_spmd.clone.sunk | while | flops 786436 | bytes 3145821 | solution.py:24
  624.8 1.7 add_select_fusion.4
  631.4 1.6 add_select_fusion.4
  633.0 1.6 add_select_fusion.4
  636.2 3.9 copy.41
  640.2 4.1 fusion.20
  644.2 7.6 %fusion.3 = bf16[16,128,512]{2,1,0:T(8,128)(2,1)S(1)} fusion(f32[16,128,512]{2,1,0:T(8,128)} %fusion.20, bf16[16,512,512]{2,1,0:T(8,128)(2,1)} %select_convert_fusion.1, bf16[512,16,128]{2,1,0:T(8,128)(2,1)S(1)} %bitcast.70), kind=kOutput, calls=%fused_computation.11 | convolution fusion | flops 1075838976 | bytes 16777216 | tf_op jit(solution)/shard_map/bhts,bshe->bthe/dot_general | solution.py:65
  651.8 2.4 copy.39
  654.2 2.7 fusion.10
  656.9 6.7 fusion.2
  663.6 3.9 copy.40
  667.5 24.4 %reduce-scatter.5.cloned.1.call-done = f32[256,256]{0,1:T(8,128)} async-done(((f32[256,2048]{0,1:T(8,128)}), f32[256,256]{0,1:T(8,128)}) %reduce-scatter.5.cloned.1.call-update) | async-done | bytes 262160 | tf_op jit(solution)/shard_map/reduce_scatter | solution.py:87
  (56 shorter events, 43.2 us)
Async XLA Ops:
  7.2 103.1 %all-gather.7.cloned.1.call-start = ((), (), s32[]{:S(2)}) async-start(), calls=%async_computation.5 | async-start | bytes 17825792 | tf_op jit(solution)/shard_map/all_gather | solution.py:14
  12.3 1.4 copy-start.3
  16.0 503.9 %reduce-scatter.3.cloned.1.call-start = ((), (), s32[]{:S(2)}) async-start(), calls=%async_computation.2 | async-start | bytes 35651584 | tf_op jit(solution)/shard_map/reduce_scatter | solution.py:79
  146.1 1.9 copy-start
  148.0 3.9 copy-start.7
  148.0 5.2 copy-start.9
  151.9 1.3 copy-start.5
  167.7 444.2 %all-gather.5.cloned.1.call-start = ((), (), s32[]{:S(2)}) async-start(), calls=%async_computation.4 | async-start | bytes 17825792 | tf_op jit(solution)/shard_map/all_gather | solution.py:14
  167.9 3.7 copy-start.1
  170.3 1.4 copy-start.6
  174.6 517.3 %reduce-scatter.5.cloned.1.call-start = ((), (), s32[]{:S(2)}) async-start(), calls=%async_computation.3 | async-start | bytes 2359296 | tf_op jit(solution)/shard_map/reduce_scatter | solution.py:87
  640.2 4.1 copy-start.2
  651.8 2.4 copy-start.8
  654.2 2.7 copy-start.4
Sparse Core Ops, SparseCore 0:
  16.1 94.1 all-gather.6
  167.8 352.0 reduce-scatter.2
  521.6 90.2 all-gather.4
  615.5 76.3 reduce-scatter.4
where the time goes:
time: 702 us; the launch traced here: 700 us
  waiting for transfers between devices  537 us (76%)
  matrix products  60.3 us (9%)
  other arithmetic  50.3 us (7%)
  local copies, waits for them, and re-layouts  38.1 us (5%)
  between operations  13.9 us (2%)
    reduce_scatter x1, waiting for transfers between devices, per_device(): lax.psum_scatter(lax.dot_general(input_rows, value_rows, (((0,), (0,)), (...  338 us
    all_gather x2, waiting for transfers between devices, prefix(): pieces = lax.all_gather(value, axis)  175 us
    select_n x30, other arithmetic, step(): return jnp.where(position < mine, longer, total)  47.8 us
    reduce_scatter x1, waiting for transfers between devices, per_device(): lax.psum_scatter(seq_total, 'grp', scatter_dimension=1, tiled=True)  24.4 us
    unnamed x27, local copies, waits for them, and re-layouts  23.6 us
    dot_general x1, matrix products, per_device(): lax.dot_general(input_rows, value_rows, (((0,), (0,)), ((), ())), preferr...  14.5 us
  transfers between devices with their start and end apart: 4, of which 4 were waited for; matrix products, arithmetic and copies ran while one was open for 11% of the time, Pallas kernels for 0%

commit v1 on v0

--- a/solution.py
+++ b/solution.py
@@ -1,12 +1,304 @@
 import jax
 import jax.numpy as jnp
 from jax import lax
+from jax.experimental import pallas as pl
+from jax.experimental.pallas import tpu as pltpu
 from jax.sharding import PartitionSpec as P
 
+MESH = pl.DeviceIdType.MESH
 H = 16
 HDIM = 128
 BLK = 512
 HD = 2048
+F32 = jnp.float32
+BF16 = jnp.bfloat16
+
+ROWS = {
+    (0, 0): (48, 40), (0, 1): (40, 48), (0, 2): (40, 40),
+    (1, 0): (40, 48), (1, 1): (48, 40), (1, 2): (40, 40),
+}
+ORDER = (("x", "y", "z"), ("y", "z", "x"), ("z", "x", "y"))
+UNITS = [(h, c, f) for h in range(2) for c in range(3) for f in range(2)]
+
+
+def row_start(h, c, f):
+    start = sum(sum(ROWS[(h, prior)]) for prior in range(c))
+    return start + (ROWS[(h, c)][0] if f else 0)
+
+
+def place():
+    seq, grp = lax.axis_index("seq"), lax.axis_index("grp")
+    core = lax.rem(seq, 2)
+    y_lo = lax.rem(lax.div(seq, 2), 2)
+    return {
+        "x": lax.rem(grp, 4),
+        "y": lax.div(grp, 4) * 2 + y_lo,
+        "z": lax.div(seq, 4),
+        "core": core,
+    }
+
+
+def device(at):
+    return (
+        at["z"] * 4 + lax.rem(at["y"], 2) * 2 + at["core"],
+        lax.div(at["y"], 2) * 4 + at["x"],
+    )
+
+
+def shifted(at, axis, delta):
+    moved = dict(at)
+    moved[axis] = lax.rem(at[axis] + delta + 4, 4)
+    return device(moved)
+
+
+def partner_of(at):
+    moved = dict(at)
+    moved["core"] = 1 - at["core"]
+    return device(moved)
+
+
+def greet(devices):
+    barrier = pltpu.get_barrier_semaphore()
+    for other in devices:
+        pl.semaphore_signal(barrier, inc=1, device_id=other, device_id_type=MESH)
+    pl.semaphore_wait(barrier, len(devices))
+
+
+def weight_kernel(xt_ref, dv_ref, out_ref, *scratch):
+    parts = {unit: scratch[4 * i] for i, unit in enumerate(UNITS)}
+    landing = {unit: scratch[4 * i + 1 : 4 * i + 4] for i, unit in enumerate(UNITS)}
+    send_sem, recv_sem = scratch[4 * len(UNITS) :]
+    at = place()
+    greet([shifted(at, axis, delta) for axis in "xyz" for delta in (1, -1)])
+
+    def view(unit, stage):
+        ref = parts[unit]
+        for earlier in range(stage):
+            ref = ref.at[at[ORDER[unit[1]][earlier]]]
+        return ref
+
+    def hop(unit, stage, kind):
+        index = UNITS.index(unit)
+        axis = ORDER[unit[1]][stage]
+        sign = 1 if unit[2] else -1
+        mine = at[axis]
+        chunk, toward = (
+            (lax.rem(mine + 2, 4), sign),
+            (lax.rem(mine - sign + 4, 4), -sign),
+            (lax.rem(mine + sign + 4, 4), sign),
+        )[kind]
+        return pltpu.make_async_remote_copy(
+            src_ref=view(unit, stage).at[chunk],
+            dst_ref=landing[unit][stage].at[kind],
+            send_sem=send_sem.at[index, stage, kind],
+            recv_sem=recv_sem.at[index, stage, kind],
+            device_id=shifted(at, axis, toward),
+            device_id_type=MESH,
+        )
+
+    def compute(h):
+        def block(b, carry):
+            rows = pl.multiple_of(b * 256, 256)
+            z, y_lo = lax.div(b, 2), lax.rem(b, 2)
+            lhs = xt_ref[pl.ds(rows, 256), :]
+            for pair in range(4):
+                acc = jnp.dot(
+                    lhs,
+                    dv_ref[h, :, pair * 256 : pair * 256 + 256],
+                    preferred_element_type=F32,
+                )
+                for side in range(2):
+                    tile = 2 * pair + side
+                    dest = {"x": tile % 4, "y": (tile // 4) * 2 + y_lo, "z": z}
+                    for c in range(3):
+                        for f in range(2):
+                            start = row_start(h, c, f)
+                            i, j, k = (dest[axis] for axis in ORDER[c])
+                            parts[(h, c, f)][i, j, k] = acc[
+                                start : start + ROWS[(h, c)][f],
+                                side * 128 : side * 128 + 128,
+                            ]
+            return carry
+
+        lax.fori_loop(0, 8, block, 0)
+
+    def units_of(h):
+        return [unit for unit in UNITS if unit[0] == h]
+
+    def issue(h, stage):
+        for kind in range(2):
+            for unit in units_of(h):
+                hop(unit, stage, kind).start()
+
+    def combine(h, stage):
+        for unit in units_of(h):
+            axis = ORDER[unit[1]][stage]
+            sign = 1 if unit[2] else -1
+            hop(unit, stage, 0).wait_recv()
+            target = view(unit, stage).at[lax.rem(at[axis] + sign + 4, 4)]
+            arrived = landing[unit][stage].at[0]
+            if stage == 0:
+                def add(i, carry, target=target, arrived=arrived):
+                    target[i] = target[i] + arrived[i]
+                    return carry
+
+                lax.fori_loop(0, 4, add, 0)
+            else:
+                target[...] = target[...] + arrived[...]
+            hop(unit, stage, 2).start()
+
+    def final(h, stage, then):
+        for unit in units_of(h):
+            axis = ORDER[unit[1]][stage]
+            hop(unit, stage, 1).wait_recv()
+            hop(unit, stage, 2).wait_recv()
+            target = view(unit, stage).at[at[axis]]
+            direct = landing[unit][stage].at[1]
+            summed = landing[unit][stage].at[2]
+            if stage == 0:
+                def add(i, carry, target=target, direct=direct, summed=summed):
+                    target[i] = target[i] + direct[i] + summed[i]
+                    return carry
+
+                lax.fori_loop(0, 4, add, 0)
+            elif stage == 1:
+                target[...] = target[...] + direct[...] + summed[...]
+            else:
+                start = row_start(*unit)
+                total = target[...] + direct[...] + summed[...]
+                out_ref[start : start + ROWS[unit[:2]][unit[2]], h * 128 : h * 128 + 128] = (
+                    total * SCALE
+                )
+            if then:
+                hop(unit, stage + 1, 0).start()
+                hop(unit, stage + 1, 1).start()
+
+    compute(0)
+    issue(0, 0)
+    compute(1)
+    combine(0, 0)
+    issue(1, 0)
+    final(0, 0, True)
+    combine(1, 0)
+    combine(0, 1)
+    final(0, 1, True)
+    final(1, 0, True)
+    combine(0, 2)
+    final(0, 2, False)
+    combine(1, 1)
+    final(1, 1, True)
+    combine(1, 2)
+    final(1, 2, False)
+    for unit in UNITS:
+        for stage in range(3):
+            for kind in range(3):
+                hop(unit, stage, kind).wait_send()
+
+
+SCALE = 65536.0 ** -0.5
+
+
+def weight(xt, dvh):
+    scratch = []
+    for h, c, f in UNITS:
+        r = ROWS[(h, c)][f]
+        scratch.append(pltpu.VMEM((4, 4, 4, r, 128), F32))
+        scratch.append(pltpu.VMEM((3, 4, 4, r, 128), F32))
+        scratch.append(pltpu.VMEM((3, 4, r, 128), F32))
+        scratch.append(pltpu.VMEM((3, r, 128), F32))
+    scratch.append(pltpu.SemaphoreType.DMA((len(UNITS), 3, 3)))
+    scratch.append(pltpu.SemaphoreType.DMA((len(UNITS), 3, 3)))
+    return pl.pallas_call(
+        weight_kernel,
+        out_shape=jax.ShapeDtypeStruct((256, 256), F32),
+        in_specs=[pl.BlockSpec(memory_space=pltpu.VMEM)] * 2,
+        out_specs=pl.BlockSpec(memory_space=pltpu.VMEM),
+        scratch_shapes=scratch,
+        compiler_params=pltpu.CompilerParams(
+            collective_id=1, has_side_effects=True, vmem_limit_bytes=60 << 20
+        ),
+        name="weight_rs",
+    )(xt, dvh)
+
+
+def pair_kernel(x_ref, dv_ref, xt_ref, dvh_ref, xs, xr, ds, dr, send_sem, recv_sem):
+    at = place()
+    core = at["core"]
+    other = partner_of(at)
+    greet([other])
+
+    def copy_x(b):
+        return pltpu.make_async_remote_copy(
+            src_ref=xs.at[b], dst_ref=xr.at[b], send_sem=send_sem.at[b],
+            recv_sem=recv_sem.at[b], device_id=other, device_id_type=MESH)
+
+    def copy_d(h):
+        return pltpu.make_async_remote_copy(
+            src_ref=ds.at[h], dst_ref=dr.at[h], send_sem=send_sem.at[8 + h],
+            recv_sem=recv_sem.at[8 + h], device_id=other, device_id_type=MESH)
+
+    for h in range(2):
+        for j in range(8):
+            piece = dv_ref[:, (2 * j + h) * 128 : (2 * j + h) * 128 + 128]
+            ds[h, :, j * 128 : j * 128 + 128] = piece.astype(F32)
+            dvh_ref[h, 0:512, j * 128 : j * 128 + 128] = piece
+        copy_d(h).start()
+
+    def send_x(b, carry):
+        cols = pl.multiple_of(b * 512 + (1 - core) * 256, 256)
+        xs[b] = x_ref[:, pl.ds(cols, 256)].astype(F32)
+        copy_x(b).start()
+        return carry
+
+    lax.fori_loop(0, 8, send_x, 0)
+
+    def own_x(b, carry):
+        cols = pl.multiple_of(b * 512 + core * 256, 256)
+        rows = pl.multiple_of(b * 256, 256)
+        xt_ref[pl.ds(rows, 256), 0:512] = x_ref[:, pl.ds(cols, 256)].T
+        return carry
+
+    lax.fori_loop(0, 8, own_x, 0)
+
+    def got_x(b, carry):
+        copy_x(b).wait_recv()
+        rows = pl.multiple_of(b * 256, 256)
+        xt_ref[pl.ds(rows, 256), 512:1024] = xr[b].astype(BF16).T
+        return carry
+
+    lax.fori_loop(0, 8, got_x, 0)
+    for h in range(2):
+        copy_d(h).wait_recv()
+        dvh_ref[h, 512:1024, :] = dr[h].astype(BF16)
+    for h in range(2):
+        copy_d(h).wait_send()
+
+    def sent_x(b, carry):
+        copy_x(b).wait_send()
+        return carry
+
+    lax.fori_loop(0, 8, sent_x, 0)
+
+
+def pair(x, dv):
+    return pl.pallas_call(
+        pair_kernel,
+        out_shape=(
+            jax.ShapeDtypeStruct((2048, 1024), BF16),
+            jax.ShapeDtypeStruct((2, 1024, 1024), BF16),
+        ),
+        in_specs=[pl.BlockSpec(memory_space=pltpu.VMEM)] * 2,
+        out_specs=(pl.BlockSpec(memory_space=pltpu.VMEM),) * 2,
+        scratch_shapes=[
+            pltpu.VMEM((8, 512, 256), F32), pltpu.VMEM((8, 512, 256), F32),
+            pltpu.VMEM((2, 512, 1024), F32), pltpu.VMEM((2, 512, 1024), F32),
+            pltpu.SemaphoreType.DMA((10,)), pltpu.SemaphoreType.DMA((10,)),
+        ],
+        compiler_params=pltpu.CompilerParams(
+            collective_id=2, has_side_effects=True, vmem_limit_bytes=60 << 20
+        ),
+        name="pair",
+    )(x, dv)
 
 
 def prefix(value, axis, join, neutral, backward):
@@ -76,17 +368,8 @@
     grad_values = grad_v.astype(jnp.bfloat16).reshape(1, tok_rows, HD)
     input_rows = layer_input[0]
     value_rows = grad_values[0]
-    seq_total = lax.psum_scatter(
-        lax.dot_general(
-            input_rows, value_rows, (((0,), (0,)), ((), ())), preferred_element_type=jnp.float32
-        ),
-        "seq",
-        scatter_dimension=0,
-        tiled=True,
-    )
-    weight_share = lax.psum_scatter(seq_total, "grp", scatter_dimension=1, tiled=True)
-    token_total = tok_rows * lax.axis_size("seq") * lax.axis_size("grp")
-    grad_weight = weight_share * float(token_total) ** (-0.5)
+    xt, dvh = pair(input_rows, value_rows)
+    grad_weight = weight(xt, dvh)
     return (grad_queries, grad_keys, grad_values, grad_weight)
 
 

time: 702 us -> 349 us (0.50)
  waiting for transfers between devices: 537 us -> 69.8 us
  Pallas kernels: 0 us -> 125 us
  matrix products: 60.3 us -> 51.2 us
    reduce_scatter x2 -> x0, waiting for transfers between devices: 362 us -> none  [the longest x1 338 us: per_device(): lax.psum_scatter(lax.dot_general(input_rows, value_rows, (((0,), (0,)), (...]
    pallas_call x0 -> x2, Pallas kernels: none -> 125 us  [the longest x1 103 us: weight(): pl.pallas_call(weight_kernel, out_shape=jax.ShapeDtypeStruct((256, 256),...]
    all_gather x2, waiting for transfers between devices: 175 us -> 69.8 us  [prefix(): pieces = lax.all_gather(value, axis)]
    dot_general x1 -> x0, matrix products: 14.5 us -> none  [per_device(): lax.dot_general(input_rows, value_rows, (((0,), (0,)), ((), ())), preferr...]
    unnamed x27 -> x31, local copies, waits for them, and re-layouts: 23.6 us -> 21.2 us
  transfers between devices with their start and end apart: 4 -> 2, of which waited for: 4 -> 1; matrix products, arithmetic and copies ran while one was open for 11% -> 21% of each run, Pallas kernels for 0% -> 36%
where the time goes in v1:
time: 349 us; the launch traced here: 348 us
  Pallas kernels  125 us (36%)
  waiting for transfers between devices  69.8 us (20%)
  matrix products  51.2 us (15%)
  other arithmetic  48.5 us (14%)
  local copies, waits for them, and re-layouts  38.1 us (11%)
  between operations  14.3 us (4%)
    pallas_call x1, Pallas kernels, weight(): pl.pallas_call(weight_kernel, out_shape=jax.ShapeDtypeStruct((256, 256),...  103 us
    all_gather x2, waiting for transfers between devices, prefix(): pieces = lax.all_gather(value, axis)  69.8 us
    select_n x30, other arithmetic, step(): return jnp.where(position < mine, longer, total)  48.3 us
    pallas_call x1, Pallas kernels, pair(): pl.pallas_call(pair_kernel, out_shape=(jax.ShapeDtypeStruct((2048, 1024),...  22.2 us
    unnamed x31, local copies, waits for them, and re-layouts  21.2 us
    rev x1, local copies, waits for them, and re-layouts, prefix(): pieces = pieces[::-1]  11.6 us
    dot_general x1, matrix products, per_device(): jnp.einsum('bhts,bshe->bthe', back, k_blocks, preferred_element_type=jnp....  8.79 us
    dot_general x1, matrix products, per_device(): jnp.einsum('bhts,bthf->bshf', within, g_blocks, preferred_element_type=jn...  8.64 us
  transfers between devices with their start and end apart: 2, of which 1 were waited for; matrix products, arithmetic and copies ran while one was open for 21% of the time, Pallas kernels for 36%

profile of v1, /device:TPU:0, one launch (start us, length us, event | category | flops | bytes accessed | tf_op | source)
XLA Modules:
  0.0 347.7 jit_solution(16113656656006033935)
XLA Ops:
  7.2 2.9 copy.46
  10.1 3.0 copy.49
  14.4 2.2 fusion.4
  16.7 2.4 copy.48
  21.1 3.0 fusion.11
  24.2 8.3 %select_convert_fusion.1 = bf16[16,512,512]{2,1,0:T(8,128)(2,1)} fusion(bf16[512,16,128]{0,2,1:T(8,128)(2,1)} %bitcast.61, pred[512,512]{1,0:T(8,128)(4,1)S(1)} %iota_compare_fusion, bf16[512,16,128]{2,1,0:T(8,128)(2,1)} %bitcast.73), kind=kOutput, calls=%fused_computation.3 | convolution fusion | flops 1082130432 | bytes 12845056 | tf_op jit(solution)/shard_map/bthf,bshf->bhts/dot_general | solution.py:354
  32.5 8.6 %fusion.3 = f32[16,512,128]{1,2,0:T(8,128)} fusion(bf16[512,16,128]{0,2,1:T(8,128)(2,1)} %bitcast.62, pred[512,512]{1,0:T(8,128)(4,1)S(1)} %iota_compare_fusion, bf16[512,16,128]{2,1,0:T(8,128)(2,1)} %bitcast.69, bf16[512,16,128]{2,1,0:T(8,128)(2,1)} %bitcast.65), kind=kOutput, calls=%fused_computation.10 | convolution fusion | flops 2155872256 | bytes 10747904 | tf_op jit(solution)/shard_map/bhts,bthf->bshf/dot_general | solution.py:363
  41.2 69.8 %all-gather.7.cloned.1.call-done = f32[256,128,128]{2,1,0:T(8,128)} async-done(((f32[16,128,128]{2,1,0:T(8,128)}), f32[256,128,128]{2,1,0:T(8,128)}) %all-gather.7.cloned.1.call-update) | async-done | bytes 16777232 | tf_op jit(solution)/shard_map/all_gather | solution.py:306
  111.0 11.6 %rev.3 = f32[16,16,128,128]{3,2,1,0:T(8,128)} reverse(f32[16,16,128,128]{3,2,1,0:T(8,128)} %bitcast.71), dimensions={0} | reverse | bytes 33554432 | tf_op jit(solution)/shard_map/rev | solution.py:308
  122.6 24.7 %while.29 = (s32[]{:T(128)}, f32[16,128,128]{2,1,0:T(8,128)S(1)}, s32[]{:T(128)}, f32[16,16,128,128]{3,2,1,0:T(8,128)}, s32[]{:T(128)}, /*index=5*/s32[]{:T(128)}) while((s32[]{:T(128)}, f32[16,128,128]{2,1,0:T(8,128)S(1)}, s32[]{:T(128)}, f32[16,16,128,128]{3,2,1,0:T(8,128)}, s32[]{:T(128)}, /*index=5*/s32[]{:T(128)}) %tuple.68), condition=%wide.region_3.4_spmd.clone, body=%wide.region_2.3_spmd.clone.sunk | while | flops 786436 | bytes 3145821 | solution.py:316
  122.6 1.8 add_select_fusion.5
  124.4 1.6 add_select_fusion.5
  129.2 1.6 add_select_fusion.5
  130.9 1.7 add_select_fusion.5
  134.2 1.6 add_select_fusion.5
  137.5 1.6 add_select_fusion.5
  140.7 1.6 add_select_fusion.5
  142.3 1.7 add_select_fusion.5
  145.7 1.6 add_select_fusion.5
  148.9 3.8 %fusion = bf16[16,128,512]{2,1,0:T(8,128)(2,1)S(1)} fusion(f32[16,512,128]{1,2,0:T(8,128)} %fusion.3, bf16[16,128,128]{2,1,0:T(8,128)(2,1)S(1)} %add_convert_fusion, bf16[512,16,128]{2,1,0:T(8,128)(2,1)S(1)} %bitcast.66), kind=kOutput, calls=%fused_computation.5 | convolution fusion | flops 270532608 | bytes 8912896 | tf_op jit(solution)/shard_map/bshe,bhef->bshf/dot_general | solution.py:365
  152.7 2.4 copy.45.dv_ref
  155.1 22.2 %pair.1 = (bf16[2048,1024]{1,0:T(8,128)(2,1)}, bf16[2,1024,1024]{2,1,0:T(8,128)(2,1)}) custom-call(bf16[512,4096]{1,0:T(8,128)(2,1)} %bitcast.77, bf16[512,2048]{1,0:T(8,128)(2,1)} %copy.45.dv_ref), custom_call_target="tpu_custom_call" | custom-call | tf_op jit(solution)/shard_map/pair/pallas_call | solution.py:284
  177.3 102.8 %weight_rs.1 = f32[256,256]{1,0:T(8,128)} custom-call(bf16[2048,1024]{1,0:T(8,128)(2,1)} %get-tuple-element.166.xt_ref, bf16[2,1024,1024]{2,1,0:T(8,128)(2,1)} %get-tuple-element.167.dv_ref), custom_call_target="tpu_custom_call" | custom-call | tf_op jit(solution)/shard_map/weight_rs/pallas_call | solution.py:211
  280.2 2.4 copy.42
  282.5 4.7 %fusion.9 = f32[16,128,512]{2,1,0:T(8,128)} fusion(bf16[16,128,128]{2,1,0:T(8,128)(2,1)} %copy-done.9, bf16[512,16,128]{2,1,0:T(8,128)(2,1)} %bitcast.74), kind=kOutput, calls=%fused_computation.15 | convolution fusion | flops 268435456 | bytes 6815744 | tf_op jit(solution)/shard_map/bshf,bhef->bshe/dot_general | solution.py:362
  287.2 24.3 %while.28 = (s32[]{:T(128)}, f32[16,128,128]{2,1,0:T(8,128)S(1)}, s32[]{:T(128)}, f32[16,16,128,128]{3,2,1,0:T(8,128)}, s32[]{:T(128)}, /*index=5*/s32[]{:T(128)}) while((s32[]{:T(128)}, f32[16,128,128]{2,1,0:T(8,128)S(1)}, s32[]{:T(128)}, f32[16,16,128,128]{3,2,1,0:T(8,128)}, s32[]{:T(128)}, /*index=5*/s32[]{:T(128)}) %tuple.77), condition=%wide.region_1.0_spmd.clone, body=%wide.region_0.0_spmd.clone.sunk | while | flops 786436 | bytes 3145821 | solution.py:316
  287.2 1.7 add_select_fusion.4
  311.6 4.0 %fusion.19 = f32[16,128,512]{2,1,0:T(8,128)} fusion(bf16[512,16,128]{0,2,1:T(8,128)(2,1)S(1)} %bitcast.63, f32[16,128,128]{2,1,0:T(8,128)S(1)} %get-tuple-element.164, f32[16,128,128]{2,1,0:T(8,128)} %fusion.11), kind=kOutput, calls=%fused_computation.27 | convolution fusion | flops 269221888 | bytes 8388608 | tf_op jit(solution)/shard_map/bthf,bhef->bthe/dot_general | solution.py:359
  315.6 8.8 %fusion.2 = bf16[16,128,512]{2,1,0:T(8,128)(2,1)} fusion(f32[16,128,512]{2,1,0:T(8,128)} %fusion.19, bf16[16,512,512]{2,1,0:T(8,128)(2,1)} %select_convert_fusion.1, bf16[512,16,128]{2,1,0:T(8,128)(2,1)S(1)} %bitcast.67), kind=kOutput, calls=%fused_computation.9 | convolution fusion | flops 1075838976 | bytes 16777216 | tf_op jit(solution)/shard_map/bhts,bshe->bthe/dot_general | solution.py:357
  324.4 4.1 %copy.40 = bf16[1,512,2048]{2,1,0:T(8,128)(2,1)} copy(bf16[1,512,2048]{1,2,0:T(8,128)(2,1)} %bitcast.76) | data formatting | bytes 4194304
  328.4 7.8 %fusion.1 = bf16[16,128,512]{2,1,0:T(8,128)(2,1)} fusion(f32[16,128,512]{2,1,0:T(8,128)} %fusion.9, bf16[16,512,512]{2,1,0:T(8,128)(2,1)} %select_convert_fusion.1, bf16[512,16,128]{2,1,0:T(8,128)(2,1)S(1)} %bitcast.70), kind=kOutput, calls=%fused_computation.7 | convolution fusion | flops 1075838976 | bytes 16777216 | tf_op jit(solution)/shard_map/bhts,bthe->bshe/dot_general | solution.py:360
  336.2 4.0 %copy.41 = bf16[1,512,2048]{2,1,0:T(8,128)(2,1)} copy(bf16[1,512,2048]{1,2,0:T(8,128)(2,1)} %bitcast.75) | data formatting | bytes 4194304
  (55 shorter events, 37.6 us)
Async XLA Ops:
  7.2 103.8 %all-gather.7.cloned.1.call-start = ((), (), s32[]{:S(2)}) async-start(), calls=%async_computation.1 | async-start | bytes 17825792 | tf_op jit(solution)/shard_map/all_gather | solution.py:306
  10.1 3.0 copy-start
  13.1 1.3 copy-start.5
  16.7 270.5 %all-gather.5.cloned.1.call-start = ((), (), s32[]{:S(2)}) async-start(), calls=%async_computation | async-start | bytes 17825792 | tf_op jit(solution)/shard_map/all_gather | solution.py:306
  16.7 2.4 copy-start.10
  19.1 1.3 copy-start.2
  19.7 1.4 copy-start.8
  122.6 24.7 %copy-start.7 = (f32[16,128,128]{2,1,0:T(8,128)S(1)}, f32[16,128,128]{2,1,0:T(8,128)}, u32[]{:S(2)}) copy-start(f32[16,128,128]{2,1,0:T(8,128)} %fusion.4) | copy-start | bytes 3145732
  147.3 1.6 copy-start.3
  148.9 3.8 %copy-start.9 = (bf16[16,128,128]{2,1,0:T(8,128)(2,1)}, bf16[16,128,128]{2,1,0:T(8,128)(2,1)S(1)}, u32[]{:S(2)}) copy-start(bf16[16,128,128]{2,1,0:T(8,128)(2,1)S(1)} %add_convert_fusion) | copy-start | bytes 1572868
  287.2 24.3 %copy-start.1 = (bf16[1,512,2048]{1,2,0:T(8,128)(2,1)S(1)}, bf16[1,512,2048]{1,2,0:T(8,128)(2,1)}, u32[]{:S(2)}) copy-start(bf16[1,512,2048]{1,2,0:T(8,128)(2,1)} %copy-done) | copy-start | bytes 6291460
  311.5 4.0 %copy-start.4 = (bf16[64,8,16,128]{3,2,1,0:T(8,128)(2,1)S(1)}, bf16[64,8,16,128]{3,2,1,0:T(8,128)(2,1)}, u32[]{:S(2)}) copy-start(bf16[64,8,16,128]{3,2,1,0:T(8,128)(2,1)} %copy-done.2) | copy-start | bytes 6291460
  324.4 4.1 %copy-start.6 = (bf16[64,8,16,128]{3,2,1,0:T(8,128)(2,1)S(1)}, bf16[64,8,16,128]{3,2,1,0:T(8,128)(2,1)}, u32[]{:S(2)}) copy-start(bf16[64,8,16,128]{3,2,1,0:T(8,128)(2,1)} %copy-done.5) | copy-start | bytes 6291460
  336.2 4.0 %copy-start.11 = (f32[256,256]{1,0:T(8,128)S(1)}, f32[256,256]{1,0:T(8,128)}, u32[]{:S(2)}) copy-start(f32[256,256]{1,0:T(8,128)} %weight_rs.1) | copy-start | bytes 786436
Sparse Core Ops, SparseCore 0:
  16.8 94.1 all-gather.6
  112.7 103.9 all-gather.4

commit v2 on v1

--- a/solution.py
+++ b/solution.py
@@ -221,156 +221,329 @@
     )(xt, dvh)
 
 
-def pair_kernel(x_ref, dv_ref, xt_ref, dvh_ref, xs, xr, ds, dr, send_sem, recv_sem):
+def grads_kernel(
+    x_hbm, q_hbm, k_hbm, v_hbm, g_hbm,
+    gq_hbm, gk_hbm, gv_hbm, xt_ref, dvh_ref,
+    qb, kb, vb, gb, sums, paired, zgot, zsend, ygot, ysend, fgot, fsend, state,
+    gq, gk, gv, xb, xs, xr, ds, dr,
+    load_sem, xload_sem, out_sem, pair_sems, z_sems, y_sems, f_sems, x_sems, d_sems,
+):
     at = place()
     core = at["core"]
+    z = at["z"]
+    y_lo = lax.rem(at["y"], 2)
     other = partner_of(at)
-    greet([other])
-
-    def copy_x(b):
+    beside = dict(at)
+    beside["y"] = at["y"] + 1 - 2 * y_lo
+    beside = device(beside)
+
+    loads = [
+        pltpu.make_async_copy(src, dst, load_sem.at[i])
+        for i, (src, dst) in enumerate(
+            ((q_hbm, qb), (g_hbm, gb), (k_hbm, kb), (v_hbm, vb))
+        )
+    ]
+    for load in loads:
+        load.start()
+
+    def load_x(b):
+        cols = pl.multiple_of(b * 512, 512)
+        slot = lax.rem(b, 2)
+        return pltpu.make_async_copy(
+            x_hbm.at[:, pl.ds(cols, 512)], xb.at[slot], xload_sem.at[slot]
+        )
+
+    load_x(0).start()
+    load_x(1).start()
+
+    def remote(src, dst, sems, index, target):
+        send, recv = sems
+        for i in index:
+            send, recv = send.at[i], recv.at[i]
         return pltpu.make_async_remote_copy(
-            src_ref=xs.at[b], dst_ref=xr.at[b], send_sem=send_sem.at[b],
-            recv_sem=recv_sem.at[b], device_id=other, device_id_type=MESH)
-
-    def copy_d(h):
-        return pltpu.make_async_remote_copy(
-            src_ref=ds.at[h], dst_ref=dr.at[h], send_sem=send_sem.at[8 + h],
-            recv_sem=recv_sem.at[8 + h], device_id=other, device_id_type=MESH)
-
-    for h in range(2):
-        for j in range(8):
-            piece = dv_ref[:, (2 * j + h) * 128 : (2 * j + h) * 128 + 128]
-            ds[h, :, j * 128 : j * 128 + 128] = piece.astype(F32)
-            dvh_ref[h, 0:512, j * 128 : j * 128 + 128] = piece
-        copy_d(h).start()
-
-    def send_x(b, carry):
-        cols = pl.multiple_of(b * 512 + (1 - core) * 256, 256)
-        xs[b] = x_ref[:, pl.ds(cols, 256)].astype(F32)
-        copy_x(b).start()
+            src_ref=src, dst_ref=dst, send_sem=send, recv_sem=recv,
+            device_id=target, device_id_type=MESH,
+        )
+
+    def pair_copy(st, j):
+        return remote(sums.at[st, 1 - core, j], paired.at[st, j], pair_sems, (st, j), other)
+
+    def z_copy(st, j):
+        return remote(
+            zsend.at[st, j], zgot.at[st, j], z_sems, (st, j),
+            shifted(at, "z", 1 if st else -1),
+        )
+
+    def y_copy(st, j):
+        return remote(ysend.at[st, j], ygot.at[st, j], y_sems, (st, j), beside)
+
+    def f_copy(st, j):
+        return remote(fsend.at[st, j], fgot.at[st, j], f_sems, (st, j), other)
+
+    def x_copy(b):
+        return remote(xs.at[lax.rem(b, 2)], xr.at[b], x_sems, (b,), other)
+
+    def d_copy(head):
+        return remote(ds.at[head], dr.at[head], d_sems, (head,), other)
+
+    for st in range(2):
+        @pl.when(z == (0 if st else 3))
+        def _(st=st):
+            zgot[st] = jnp.zeros((8, HDIM, HDIM), F32)
+
+    greet([other, beside, shifted(at, "z", 1), shifted(at, "z", -1)])
+
+    def lanes(head):
+        return pl.ds(pl.multiple_of(head * HDIM, HDIM), HDIM)
+
+    def outer(lhs, rhs, head):
+        return lax.dot_general(
+            lhs[:, lanes(head)], rhs[:, lanes(head)], (((0,), (0,)), ((), ())),
+            preferred_element_type=F32,
+        )
+
+    def sum_states(st, lhs, rhs):
+        def theirs(j, carry):
+            sums[st, 1 - core, j] = outer(lhs, rhs, (1 - core) * 8 + j)
+            pair_copy(st, j).start()
+            return carry
+
+        def mine(j, carry):
+            sums[st, core, j] = outer(lhs, rhs, core * 8 + j)
+            return carry
+
+        lax.fori_loop(0, 8, theirs, 0)
+        lax.fori_loop(0, 8, mine, 0)
+
+    loads[0].wait()
+    loads[1].wait()
+    sum_states(0, qb, gb)
+    loads[2].wait()
+    loads[3].wait()
+    sum_states(1, kb, vb)
+
+    def chain(st, j):
+        pair_copy(st, j).wait_recv()
+
+        @pl.when(z != (0 if st else 3))
+        def _():
+            z_copy(st, j).wait_recv()
+
+        chip = sums[st, core, j] + paired[st, j]
+        far = zgot[st, j]
+        zsend[st, j] = chip + far
+        full = y_lo == (0 if st else 1)
+        ysend[st, j] = far + jnp.where(full, chip, 0.0)
+
+        @pl.when(z != (3 if st else 0))
+        def _():
+            z_copy(st, j).start()
+
+        y_copy(st, j).start()
+
+    def settle(st, j):
+        y_copy(st, j).wait_recv()
+        both = zgot[st, j] + ygot[st, j]
+        inner = 1 if st else 0
+        fsend[st, j] = both + jnp.where(core != inner, sums[st, core, j], 0.0)
+        f_copy(st, j).start()
+        state[st, core * 8 + j] = (
+            both + jnp.where(core == inner, paired[st, j], 0.0)
+        ).astype(BF16)
+
+    def receive(st, j):
+        f_copy(st, j).wait_recv()
+        state[st, (1 - core) * 8 + j] = fgot[st, j].astype(BF16)
+
+    def nt(lhs, rhs):
+        return lax.dot_general(lhs, rhs, (((1,), (1,)), ((), ())), preferred_element_type=F32)
+
+    def nn(lhs, rhs):
+        return jnp.dot(lhs, rhs, preferred_element_type=F32)
+
+    half = 256
+    row = lax.broadcasted_iota(jnp.int32, (half, half), 0)
+    col = lax.broadcasted_iota(jnp.int32, (half, half), 1)
+
+    def lower(block):
+        return jnp.where(col <= row, block, 0.0).astype(BF16)
+
+    def upper(block):
+        return jnp.where(row <= col, block, 0.0).astype(BF16)
+
+    def local(head):
+        q, k = qb[:, lanes(head)], kb[:, lanes(head)]
+        v, g = vb[:, lanes(head)], gb[:, lanes(head)]
+        q0, q1, k0, k1 = q[:half], q[half:], k[:half], k[half:]
+        v0, v1, g0, g1 = v[:half], v[half:], g[:half], g[half:]
+        gv[head, 0:half] = nn(upper(nt(k0, q0)), g0) + nn(nt(k0, q1).astype(BF16), g1)
+        gv[head, half:BLK] = nn(upper(nt(k1, q1)), g1)
+        gk[head, 0:half] = nn(upper(nt(v0, g0)), q0) + nn(nt(v0, g1).astype(BF16), q1)
+        gk[head, half:BLK] = nn(upper(nt(v1, g1)), q1)
+        gq[head, 0:half] = nn(lower(nt(g0, v0)), k0)
+        gq[head, half:BLK] = nn(nt(g1, v0).astype(BF16), k0) + nn(lower(nt(g1, v1)), k1)
+
+    def send_x(b):
+        slot = lax.rem(b, 2)
+        load_x(b).wait()
+
+        @pl.when(b >= 2)
+        def _():
+            x_copy(b - 2).wait_send()
+
+        theirs = pl.multiple_of((1 - core) * 256, 256)
+        mine = pl.multiple_of(core * 256, 256)
+        xs[slot] = xb[slot, :, pl.ds(theirs, 256)].astype(F32)
+        x_copy(b).start()
+        rows = pl.multiple_of(b * 256, 256)
+        xt_ref[pl.ds(rows, 256), 0:BLK] = xb[slot, :, pl.ds(mine, 256)].T
+
+        @pl.when(b < 6)
+        def _():
+            load_x(b + 2).start()
+
+    def take_x(b):
+        x_copy(b).wait_recv()
+        rows = pl.multiple_of(b * 256, 256)
+        xt_ref[pl.ds(rows, 256), BLK : 2 * BLK] = xr[b].astype(BF16).T
+
+    LAG = 3
+
+    def slot_step(i, carry):
+        for st in range(2):
+            first = LAG * (z if st else 3 - z)
+            j = i - first
+
+            @pl.when(jnp.logical_and(j >= 0, j < 8))
+            def _(st=st, j=j):
+                chain(st, j)
+
+            @pl.when(jnp.logical_and(j >= LAG, j < 8 + LAG))
+            def _(st=st, j=j):
+                settle(st, j - LAG)
+
+        @pl.when(i < 8)
+        def _():
+            send_x(i)
+
+        @pl.when(jnp.logical_and(i >= 8, i < 16))
+        def _():
+            take_x(i - 8)
+
+        @pl.when(i < 16)
+        def _():
+            local(i)
+
         return carry
 
-    lax.fori_loop(0, 8, send_x, 0)
-
-    def own_x(b, carry):
-        cols = pl.multiple_of(b * 512 + core * 256, 256)
-        rows = pl.multiple_of(b * 256, 256)
-        xt_ref[pl.ds(rows, 256), 0:512] = x_ref[:, pl.ds(cols, 256)].T
-        return carry
-
-    lax.fori_loop(0, 8, own_x, 0)
-
-    def got_x(b, carry):
-        copy_x(b).wait_recv()
-        rows = pl.multiple_of(b * 256, 256)
-        xt_ref[pl.ds(rows, 256), 512:1024] = xr[b].astype(BF16).T
-        return carry
-
-    lax.fori_loop(0, 8, got_x, 0)
-    for h in range(2):
-        copy_d(h).wait_recv()
-        dvh_ref[h, 512:1024, :] = dr[h].astype(BF16)
-    for h in range(2):
-        copy_d(h).wait_send()
-
-    def sent_x(b, carry):
-        copy_x(b).wait_send()
-        return carry
-
-    lax.fori_loop(0, 8, sent_x, 0)
-
-
-def pair(x, dv):
+    lax.fori_loop(0, 8 + 4 * LAG, slot_step, 0)
+
+    def each(count, body):
+        def run(i, carry):
+            body(i)
+            return carry
+
+        lax.fori_loop(0, count, run, 0)
+
+    each(8, lambda j: receive(0, j))
+
+    def finish_v(head):
+        total = gv[head] + nn(kb[:, lanes(head)], state[0, head])
+        rounded = total.astype(BF16)
+        ds[head] = rounded.astype(F32)
+        d_copy(head).start()
+        kb[:, lanes(head)] = rounded
+        h, place_in = lax.rem(head, 2), lax.div(head, 2)
+        dvh_ref[h, 0:BLK, lanes(place_in)] = rounded
+
+    each(16, finish_v)
+    stores = [
+        pltpu.make_async_copy(src, dst, out_sem.at[i])
+        for i, (src, dst) in enumerate(((gb, gq_hbm), (vb, gk_hbm), (kb, gv_hbm)))
+    ]
+    stores[2].start()
+
+    def finish_k(head):
+        total = gk[head] + nt(vb[:, lanes(head)], state[0, head])
+        vb[:, lanes(head)] = total.astype(BF16)
+
+    each(16, finish_k)
+    stores[1].start()
+    each(8, lambda j: receive(1, j))
+
+    def finish_q(head):
+        total = gq[head] + nt(gb[:, lanes(head)], state[1, head])
+        gb[:, lanes(head)] = total.astype(BF16)
+
+    each(16, finish_q)
+    stores[0].start()
+
+    def take_d(head):
+        d_copy(head).wait_recv()
+        h, place_in = lax.rem(head, 2), lax.div(head, 2)
+        dvh_ref[h, BLK : 2 * BLK, lanes(place_in)] = dr[head].astype(BF16)
+
+    each(16, take_d)
+    each(16, lambda head: d_copy(head).wait_send())
+    each(2, lambda b: x_copy(b + 6).wait_send())
+    for st in range(2):
+        def drain(j, st=st):
+            pair_copy(st, j).wait_send()
+            y_copy(st, j).wait_send()
+            f_copy(st, j).wait_send()
+
+            @pl.when(z != (3 if st else 0))
+            def _():
+                z_copy(st, j).wait_send()
+
+        each(8, drain)
+    for store in stores:
+        store.wait()
+
+
+def grads(x, q, k, v, g):
+    wide = jax.ShapeDtypeStruct((BLK, HD), BF16)
+    dma = pltpu.SemaphoreType.DMA
+    hop = pltpu.VMEM((2, 8, HDIM, HDIM), F32)
+    partial = pltpu.VMEM((H, BLK, HDIM), F32)
+    any_spec = pl.BlockSpec(memory_space=pl.ANY)
+    vmem_spec = pl.BlockSpec(memory_space=pltpu.VMEM)
     return pl.pallas_call(
-        pair_kernel,
+        grads_kernel,
         out_shape=(
+            wide, wide, wide,
             jax.ShapeDtypeStruct((2048, 1024), BF16),
             jax.ShapeDtypeStruct((2, 1024, 1024), BF16),
         ),
-        in_specs=[pl.BlockSpec(memory_space=pltpu.VMEM)] * 2,
-        out_specs=(pl.BlockSpec(memory_space=pltpu.VMEM),) * 2,
+        in_specs=[any_spec] * 5,
+        out_specs=(any_spec,) * 3 + (vmem_spec,) * 2,
         scratch_shapes=[
-            pltpu.VMEM((8, 512, 256), F32), pltpu.VMEM((8, 512, 256), F32),
-            pltpu.VMEM((2, 512, 1024), F32), pltpu.VMEM((2, 512, 1024), F32),
-            pltpu.SemaphoreType.DMA((10,)), pltpu.SemaphoreType.DMA((10,)),
+            *[pltpu.VMEM((BLK, HD), BF16)] * 4,
+            pltpu.VMEM((2, 2, 8, HDIM, HDIM), F32),
+            *[hop] * 7,
+            pltpu.VMEM((2, H, HDIM, HDIM), BF16),
+            *[partial] * 3,
+            pltpu.VMEM((2, BLK, 512), BF16),
+            pltpu.VMEM((2, BLK, 256), F32),
+            pltpu.VMEM((8, BLK, 256), F32),
+            partial, partial,
+            dma((4,)), dma((2,)), dma((3,)),
+            *[(dma((2, 8)), dma((2, 8)))] * 4,
+            (dma((8,)), dma((8,))),
+            (dma((H,)), dma((H,))),
         ],
         compiler_params=pltpu.CompilerParams(
-            collective_id=2, has_side_effects=True, vmem_limit_bytes=60 << 20
+            collective_id=2, has_side_effects=True, vmem_limit_bytes=62 << 20
         ),
-        name="pair",
-    )(x, dv)
-
-
-def prefix(value, axis, join, neutral, backward):
-    count, mine = (lax.axis_size(axis), lax.axis_index(axis))
-    pieces = lax.all_gather(value, axis)
-    if backward:
-        pieces = pieces[::-1]
-        mine = count - 1 - mine
-    total = jnp.full_like(value, 0) + jnp.asarray(neutral, value.dtype)
-
-    def step(position, total):
-        longer = join(total, pieces[position])
-        return jnp.where(position < mine, longer, total)
-
-    return lax.fori_loop(0, count - 1, step, total)
-
-
-def add_states(earlier, later):
-    return earlier + later
+        name="grads",
+    )(x, q, k, v, g)
 
 
 def per_device(layer_input, queries, key_vectors, value_vectors, grad_output):
-    tok_rows = queries.shape[1]
-    block_len = min(tok_rows, BLK)
-    block_count = tok_rows // block_len
-
-    def split(array):
-        return array.reshape(block_count, block_len, H, HDIM)
-
-    q_blocks = split(queries)
-    k_blocks = split(key_vectors)
-    v_blocks = split(value_vectors)
-    g_blocks = split(grad_output)
-    kv_sum = jnp.einsum("bthe,bthf->bhef", k_blocks, v_blocks, preferred_element_type=jnp.float32)
-    qg_sum = jnp.einsum("bthe,bthf->bhef", q_blocks, g_blocks, preferred_element_type=jnp.float32)
-    kv_device = jnp.sum(kv_sum, axis=0)
-    qg_device = jnp.sum(qg_sum, axis=0)
-    zero_state = jnp.zeros((H, HDIM, HDIM), jnp.float32)
-    before_device = prefix(kv_device, "seq", add_states, zero_state, False)
-    after_device = prefix(qg_device, "seq", add_states, zero_state, True)
-    before = before_device + (jnp.cumsum(kv_sum, axis=0) - kv_sum)
-    after = after_device + (qg_device - jnp.cumsum(qg_sum, axis=0))
-    before_r = before.astype(jnp.bfloat16)
-    after_r = after.astype(jnp.bfloat16)
-    causal = jnp.tril(jnp.ones((block_len, block_len), dtype=bool))
-    within = jnp.where(
-        causal,
-        jnp.einsum("bthe,bshe->bhts", q_blocks, k_blocks, preferred_element_type=jnp.float32),
-        0.0,
-    ).astype(jnp.bfloat16)
-    back = jnp.where(
-        causal,
-        jnp.einsum("bthf,bshf->bhts", g_blocks, v_blocks, preferred_element_type=jnp.float32),
-        0.0,
-    ).astype(jnp.bfloat16)
-    grad_q = jnp.einsum(
-        "bhts,bshe->bthe", back, k_blocks, preferred_element_type=jnp.float32
-    ) + jnp.einsum("bthf,bhef->bthe", g_blocks, before_r, preferred_element_type=jnp.float32)
-    grad_k = jnp.einsum(
-        "bhts,bthe->bshe", back, q_blocks, preferred_element_type=jnp.float32
-    ) + jnp.einsum("bshf,bhef->bshe", v_blocks, after_r, preferred_element_type=jnp.float32)
-    grad_v = jnp.einsum(
-        "bhts,bthf->bshf", within, g_blocks, preferred_element_type=jnp.float32
-    ) + jnp.einsum("bshe,bhef->bshf", k_blocks, after_r, preferred_element_type=jnp.float32)
-    grad_queries = grad_q.astype(jnp.bfloat16).reshape(1, tok_rows, HD)
-    grad_keys = grad_k.astype(jnp.bfloat16).reshape(1, tok_rows, HD)
-    grad_values = grad_v.astype(jnp.bfloat16).reshape(1, tok_rows, HD)
-    input_rows = layer_input[0]
-    value_rows = grad_values[0]
-    xt, dvh = pair(input_rows, value_rows)
+    arrays = (layer_input, queries, key_vectors, value_vectors, grad_output)
+    gq, gk, gv, xt, dvh = grads(*(array[0] for array in arrays))
     grad_weight = weight(xt, dvh)
-    return (grad_queries, grad_keys, grad_values, grad_weight)
+    return (gq[None], gk[None], gv[None], grad_weight)
 
 
 def solution(mesh):

time: 349 us -> 158 us (0.45)
  waiting for transfers between devices: 69.8 us -> 0 us
  matrix products: 51.2 us -> 0 us
  other arithmetic: 48.5 us -> 0 us
  local copies, waits for them, and re-layouts: 38.1 us -> 6.72 us
  Pallas kernels: 125 us -> 150 us
  between operations: 14.3 us -> 0.68 us
    all_gather x2 -> x0, waiting for transfers between devices: 69.8 us -> none  [prefix(): pieces = lax.all_gather(value, axis)]
    dot_general x9 -> x0, matrix products: 51.2 us -> none  [the longest x1 8.79 us: per_device(): jnp.einsum('bhts,bshe->bthe', back, k_blocks, preferred_element_type=jnp....]
    select_n x30 -> x0, other arithmetic: 48.3 us -> none  [step(): return jnp.where(position < mine, longer, total)]
    pallas_call x1, Pallas kernels: 22.2 us -> 59.2 us  [grads(): pl.pallas_call(grads_kernel, out_shape=(wide, wide, wide, jax.ShapeDtypeS...]
    unnamed x31 -> x12, local copies, waits for them, and re-layouts: 21.2 us -> 6.72 us
    pallas_call x1, Pallas kernels: 103 us -> 90.9 us  [weight(): pl.pallas_call(weight_kernel, out_shape=jax.ShapeDtypeStruct((256, 256),...]
    rev x1 -> x0, local copies, waits for them, and re-layouts: 11.6 us -> none  [prefix(): pieces = pieces[::-1]]
  transfers between devices with their start and end apart: 2 -> 0, of which waited for: 1 -> 0; matrix products, arithmetic and copies ran while one was open for 21% -> 0% of each run, Pallas kernels for 36% -> 0%
where the time goes in v2:
time: 158 us; the launch traced here: 157 us
  Pallas kernels  150 us (95%)
  local copies, waits for them, and re-layouts  6.72 us (4%)
    pallas_call x1, Pallas kernels, weight(): pl.pallas_call(weight_kernel, out_shape=jax.ShapeDtypeStruct((256, 256),...  90.9 us
    pallas_call x1, Pallas kernels, grads(): pl.pallas_call(grads_kernel, out_shape=(wide, wide, wide, jax.ShapeDtypeS...  59.2 us
    unnamed x12, local copies, waits for them, and re-layouts  6.72 us

profile of v2, /device:TPU:0, one launch (start us, length us, event | category | flops | bytes accessed | tf_op | source)
XLA Modules:
  0.0 157.5 jit_solution(18169279146538841034)
XLA Ops:
  0.6 59.2 %grads.1 = (bf16[512,2048]{1,0:T(8,128)(2,1)}, bf16[512,2048]{1,0:T(8,128)(2,1)}, bf16[512,2048]{1,0:T(8,128)(2,1)}, bf16[2048,1024]{1,0:T(8,128)(2,1)}, bf16[2,1024,1024]{2,1,0:T(8,128)(2,1)}) custom-call(bf16[512,4096]{1,0:T(8,128)(2,1)} %bitcast.8, bf16[512,2048]{1,0:T(8,128)(2,1)} %bitcast.12, bf16[512,2048]{1,0:T(8,128)(2,1)} %bitcast.13, ...), custom_call_target="tpu_custom_call" | custom-call | tf_op jit(solution)/shard_map/grads/pallas_call | solution.py:511
  59.8 0.0 copy-start.2
  59.8 90.9 %weight_rs.1 = f32[256,256]{1,0:T(8,128)} custom-call(bf16[2048,1024]{1,0:T(8,128)(2,1)} %get-tuple-element.12.xt_ref, bf16[2,1024,1024]{2,1,0:T(8,128)(2,1)} %get-tuple-element.13.dv_ref), custom_call_target="tpu_custom_call" | custom-call | tf_op jit(solution)/shard_map/weight_rs/pallas_call | solution.py:211
  150.7 0.0 copy-done.2
  150.7 0.0 copy-start.1
  150.7 1.3 copy.13
  152.1 1.0 copy-done.1
  153.1 0.0 copy-start
  153.1 1.3 copy.14
  154.4 1.0 copy-done
  155.4 0.0 copy-start.3
  155.4 1.3 copy.15
  156.8 0.0 copy-done.3
  156.8 0.7 copy.16
Async XLA Ops:
  59.8 90.9 %copy-start.2 = (bf16[512,2048]{1,0:T(8,128)(2,1)S(1)}, bf16[512,2048]{1,0:T(8,128)(2,1)}, u32[]{:S(2)}) copy-start(bf16[512,2048]{1,0:T(8,128)(2,1)} %get-tuple-element.9) | copy-start | bytes 6291460
  150.7 2.3 %copy-start.1 = (bf16[512,2048]{1,0:T(8,128)(2,1)S(1)}, bf16[512,2048]{1,0:T(8,128)(2,1)}, u32[]{:S(2)}) copy-start(bf16[512,2048]{1,0:T(8,128)(2,1)} %get-tuple-element.10) | copy-start | bytes 6291460
  153.1 2.3 %copy-start = (bf16[512,2048]{1,0:T(8,128)(2,1)S(1)}, bf16[512,2048]{1,0:T(8,128)(2,1)}, u32[]{:S(2)}) copy-start(bf16[512,2048]{1,0:T(8,128)(2,1)} %get-tuple-element.11) | copy-start | bytes 6291460
  155.4 1.3 copy-start.3

commit v3 on v2

--- a/solution.py
+++ b/solution.py
@@ -64,7 +64,45 @@
     pl.semaphore_wait(barrier, len(devices))
 
 
-def weight_kernel(xt_ref, dv_ref, out_ref, *scratch):
+def lanes(head):
+    return pl.ds(pl.multiple_of(head * HDIM, HDIM), HDIM)
+
+
+def nt(lhs, rhs):
+    return lax.dot_general(lhs, rhs, (((1,), (1,)), ((), ())), preferred_element_type=F32)
+
+
+def nn(lhs, rhs):
+    return jnp.dot(lhs, rhs, preferred_element_type=F32)
+
+
+HALF = BLK // 2
+
+
+def lower(block):
+    row = lax.broadcasted_iota(jnp.int32, (HALF, HALF), 0)
+    col = lax.broadcasted_iota(jnp.int32, (HALF, HALF), 1)
+    return jnp.where(col <= row, block, 0.0).astype(BF16)
+
+
+def upper(block):
+    row = lax.broadcasted_iota(jnp.int32, (HALF, HALF), 0)
+    col = lax.broadcasted_iota(jnp.int32, (HALF, HALF), 1)
+    return jnp.where(row <= col, block, 0.0).astype(BF16)
+
+
+def weight_kernel(
+    xt_ref, dv_ref, state_ref, q_hbm, k_hbm, v_hbm, g_hbm,
+    out_ref, gq_hbm, gk_hbm, qb, kb, vb, gb, load_sem, store_sem, *scratch
+):
+    loads = [
+        pltpu.make_async_copy(src, dst, load_sem.at[i])
+        for i, (src, dst) in enumerate(
+            ((q_hbm, qb), (k_hbm, kb), (v_hbm, vb), (g_hbm, gb))
+        )
+    ]
+    for load in loads:
+        load.start()
     parts = {unit: scratch[4 * i] for i, unit in enumerate(UNITS)}
     landing = {unit: scratch[4 * i + 1 : 4 * i + 4] for i, unit in enumerate(UNITS)}
     send_sem, recv_sem = scratch[4 * len(UNITS) :]
@@ -173,14 +211,50 @@
                 hop(unit, stage + 1, 0).start()
                 hop(unit, stage + 1, 1).start()
 
+    def attend(head):
+        q, k = qb[:, lanes(head)], kb[:, lanes(head)]
+        v, g = vb[:, lanes(head)], gb[:, lanes(head)]
+        q0, q1, k0, k1 = q[:HALF], q[HALF:], k[:HALF], k[HALF:]
+        v0, v1, g0, g1 = v[:HALF], v[HALF:], g[:HALF], g[HALF:]
+        after, before = state_ref[0, head], state_ref[1, head]
+        gk0 = nn(upper(nt(v0, g0)), q0) + nn(nt(v0, g1).astype(BF16), q1) + nt(v0, after)
+        gk1 = nn(upper(nt(v1, g1)), q1) + nt(v1, after)
+        gq0 = nn(lower(nt(g0, v0)), k0) + nt(g0, before)
+        gq1 = (
+            nn(nt(g1, v0).astype(BF16), k0) + nn(lower(nt(g1, v1)), k1) + nt(g1, before)
+        )
+        vb[0:HALF, lanes(head)] = gk0.astype(BF16)
+        vb[HALF:BLK, lanes(head)] = gk1.astype(BF16)
+        gb[0:HALF, lanes(head)] = gq0.astype(BF16)
+        gb[HALF:BLK, lanes(head)] = gq1.astype(BF16)
+
+    def fill(first, last):
+        def run(head, carry):
+            attend(head)
+            return carry
+
+        lax.fori_loop(first, last, run, 0)
+
     compute(0)
     issue(0, 0)
     compute(1)
     combine(0, 0)
     issue(1, 0)
+    for load in loads:
+        load.wait()
+    fill(0, 6)
     final(0, 0, True)
+    fill(6, 10)
     combine(1, 0)
+    fill(10, 13)
     combine(0, 1)
+    fill(13, 16)
+    stores = [
+        pltpu.make_async_copy(gb, gq_hbm, store_sem.at[0]),
+        pltpu.make_async_copy(vb, gk_hbm, store_sem.at[1]),
+    ]
+    for store in stores:
+        store.start()
     final(0, 1, True)
     final(1, 0, True)
     combine(0, 2)
@@ -193,13 +267,20 @@
         for stage in range(3):
             for kind in range(3):
                 hop(unit, stage, kind).wait_send()
+    for store in stores:
+        store.wait()
 
 
 SCALE = 65536.0 ** -0.5
 
 
-def weight(xt, dvh):
-    scratch = []
+def weight(xt, dvh, state, q, k, v, g):
+    wide = jax.ShapeDtypeStruct((BLK, HD), BF16)
+    any_spec = pl.BlockSpec(memory_space=pl.ANY)
+    vmem_spec = pl.BlockSpec(memory_space=pltpu.VMEM)
+    scratch = [pltpu.VMEM((BLK, HD), BF16)] * 4
+    scratch.append(pltpu.SemaphoreType.DMA((4,)))
+    scratch.append(pltpu.SemaphoreType.DMA((2,)))
     for h, c, f in UNITS:
         r = ROWS[(h, c)][f]
         scratch.append(pltpu.VMEM((4, 4, 4, r, 128), F32))
@@ -210,22 +291,22 @@
     scratch.append(pltpu.SemaphoreType.DMA((len(UNITS), 3, 3)))
     return pl.pallas_call(
         weight_kernel,
-        out_shape=jax.ShapeDtypeStruct((256, 256), F32),
-        in_specs=[pl.BlockSpec(memory_space=pltpu.VMEM)] * 2,
-        out_specs=pl.BlockSpec(memory_space=pltpu.VMEM),
+        out_shape=(jax.ShapeDtypeStruct((256, 256), F32), wide, wide),
+        in_specs=[vmem_spec] * 3 + [any_spec] * 4,
+        out_specs=(vmem_spec, any_spec, any_spec),
         scratch_shapes=scratch,
         compiler_params=pltpu.CompilerParams(
             collective_id=1, has_side_effects=True, vmem_limit_bytes=60 << 20
         ),
         name="weight_rs",
-    )(xt, dvh)
+    )(xt, dvh, state, q, k, v, g)
 
 
 def grads_kernel(
     x_hbm, q_hbm, k_hbm, v_hbm, g_hbm,
-    gq_hbm, gk_hbm, gv_hbm, xt_ref, dvh_ref,
-    qb, kb, vb, gb, sums, paired, zgot, zsend, ygot, ysend, fgot, fsend, state,
-    gq, gk, gv, xb, xs, xr, ds, dr,
+    gv_hbm, xt_ref, dvh_ref, state,
+    qb, kb, vb, gb, sums, paired, zgot, zsend, ygot, ysend, fgot, fsend,
+    gv, xb, xs, xr, ds, dr,
     load_sem, xload_sem, out_sem, pair_sems, z_sems, y_sems, f_sems, x_sems, d_sems,
 ):
     at = place()
@@ -293,34 +374,33 @@
 
     greet([other, beside, shifted(at, "z", 1), shifted(at, "z", -1)])
 
-    def lanes(head):
-        return pl.ds(pl.multiple_of(head * HDIM, HDIM), HDIM)
-
     def outer(lhs, rhs, head):
         return lax.dot_general(
             lhs[:, lanes(head)], rhs[:, lanes(head)], (((0,), (0,)), ((), ())),
             preferred_element_type=F32,
         )
 
-    def sum_states(st, lhs, rhs):
-        def theirs(j, carry):
-            sums[st, 1 - core, j] = outer(lhs, rhs, (1 - core) * 8 + j)
-            pair_copy(st, j).start()
-            return carry
-
-        def mine(j, carry):
-            sums[st, core, j] = outer(lhs, rhs, core * 8 + j)
-            return carry
-
-        lax.fori_loop(0, 8, theirs, 0)
-        lax.fori_loop(0, 8, mine, 0)
-
     loads[0].wait()
     loads[1].wait()
-    sum_states(0, qb, gb)
+
+    def theirs(j, carry):
+        sums[0, 1 - core, j] = outer(qb, gb, (1 - core) * 8 + j)
+        pair_copy(0, j).start()
+        return carry
+
+    def mine(j, carry):
+        sums[0, core, j] = outer(qb, gb, core * 8 + j)
+        return carry
+
+    lax.fori_loop(0, 8, theirs, 0)
+    lax.fori_loop(0, 8, mine, 0)
     loads[2].wait()
     loads[3].wait()
-    sum_states(1, kb, vb)
+
+    def sum_keys(j):
+        sums[1, 1 - core, j] = outer(kb, vb, (1 - core) * 8 + j)
+        pair_copy(1, j).start()
+        sums[1, core, j] = outer(kb, vb, core * 8 + j)
 
     def chain(st, j):
         pair_copy(st, j).wait_recv()
@@ -355,97 +435,12 @@
         f_copy(st, j).wait_recv()
         state[st, (1 - core) * 8 + j] = fgot[st, j].astype(BF16)
 
-    def nt(lhs, rhs):
-        return lax.dot_general(lhs, rhs, (((1,), (1,)), ((), ())), preferred_element_type=F32)
-
-    def nn(lhs, rhs):
-        return jnp.dot(lhs, rhs, preferred_element_type=F32)
-
-    half = 256
-    row = lax.broadcasted_iota(jnp.int32, (half, half), 0)
-    col = lax.broadcasted_iota(jnp.int32, (half, half), 1)
-
-    def lower(block):
-        return jnp.where(col <= row, block, 0.0).astype(BF16)
-
-    def upper(block):
-        return jnp.where(row <= col, block, 0.0).astype(BF16)
-
     def local(head):
-        q, k = qb[:, lanes(head)], kb[:, lanes(head)]
-        v, g = vb[:, lanes(head)], gb[:, lanes(head)]
-        q0, q1, k0, k1 = q[:half], q[half:], k[:half], k[half:]
-        v0, v1, g0, g1 = v[:half], v[half:], g[:half], g[half:]
-        gv[head, 0:half] = nn(upper(nt(k0, q0)), g0) + nn(nt(k0, q1).astype(BF16), g1)
-        gv[head, half:BLK] = nn(upper(nt(k1, q1)), g1)
-        gk[head, 0:half] = nn(upper(nt(v0, g0)), q0) + nn(nt(v0, g1).astype(BF16), q1)
-        gk[head, half:BLK] = nn(upper(nt(v1, g1)), q1)
-        gq[head, 0:half] = nn(lower(nt(g0, v0)), k0)
-        gq[head, half:BLK] = nn(nt(g1, v0).astype(BF16), k0) + nn(lower(nt(g1, v1)), k1)
-
-    def send_x(b):
-        slot = lax.rem(b, 2)
-        load_x(b).wait()
-
-        @pl.when(b >= 2)
-        def _():
-            x_copy(b - 2).wait_send()
-
-        theirs = pl.multiple_of((1 - core) * 256, 256)
-        mine = pl.multiple_of(core * 256, 256)
-        xs[slot] = xb[slot, :, pl.ds(theirs, 256)].astype(F32)
-        x_copy(b).start()
-        rows = pl.multiple_of(b * 256, 256)
-        xt_ref[pl.ds(rows, 256), 0:BLK] = xb[slot, :, pl.ds(mine, 256)].T
-
-        @pl.when(b < 6)
-        def _():
-            load_x(b + 2).start()
-
-    def take_x(b):
-        x_copy(b).wait_recv()
-        rows = pl.multiple_of(b * 256, 256)
-        xt_ref[pl.ds(rows, 256), BLK : 2 * BLK] = xr[b].astype(BF16).T
-
-    LAG = 3
-
-    def slot_step(i, carry):
-        for st in range(2):
-            first = LAG * (z if st else 3 - z)
-            j = i - first
-
-            @pl.when(jnp.logical_and(j >= 0, j < 8))
-            def _(st=st, j=j):
-                chain(st, j)
-
-            @pl.when(jnp.logical_and(j >= LAG, j < 8 + LAG))
-            def _(st=st, j=j):
-                settle(st, j - LAG)
-
-        @pl.when(i < 8)
-        def _():
-            send_x(i)
-
-        @pl.when(jnp.logical_and(i >= 8, i < 16))
-        def _():
-            take_x(i - 8)
-
-        @pl.when(i < 16)
-        def _():
-            local(i)
-
-        return carry
-
-    lax.fori_loop(0, 8 + 4 * LAG, slot_step, 0)
-
-    def each(count, body):
-        def run(i, carry):
-            body(i)
-            return carry
-
-        lax.fori_loop(0, count, run, 0)
-
-    each(8, lambda j: receive(0, j))
+        q, k, g = qb[:, lanes(head)], kb[:, lanes(head)], gb[:, lanes(head)]
+        q0, q1, k0, k1 = q[:HALF], q[HALF:], k[:HALF], k[HALF:]
+        g0, g1 = g[:HALF], g[HALF:]
+        gv[head, 0:HALF] = nn(upper(nt(k0, q0)), g0) + nn(nt(k0, q1).astype(BF16), g1)
+        gv[head, HALF:BLK] = nn(upper(nt(k1, q1)), g1)
 
     def finish_v(head):
         total = gv[head] + nn(kb[:, lanes(head)], state[0, head])
@@ -456,27 +451,84 @@
         h, place_in = lax.rem(head, 2), lax.div(head, 2)
         dvh_ref[h, 0:BLK, lanes(place_in)] = rounded
 
-    each(16, finish_v)
-    stores = [
-        pltpu.make_async_copy(src, dst, out_sem.at[i])
-        for i, (src, dst) in enumerate(((gb, gq_hbm), (vb, gk_hbm), (kb, gv_hbm)))
-    ]
-    stores[2].start()
-
-    def finish_k(head):
-        total = gk[head] + nt(vb[:, lanes(head)], state[0, head])
-        vb[:, lanes(head)] = total.astype(BF16)
-
-    each(16, finish_k)
-    stores[1].start()
+    def send_x(b):
+        slot = lax.rem(b, 2)
+        load_x(b).wait()
+
+        @pl.when(b >= 2)
+        def _():
+            x_copy(b - 2).wait_send()
+
+        theirs = pl.multiple_of((1 - core) * 256, 256)
+        mine = pl.multiple_of(core * 256, 256)
+        xs[slot] = xb[slot, :, pl.ds(theirs, 256)].astype(F32)
+        x_copy(b).start()
+        rows = pl.multiple_of(b * 256, 256)
+        xt_ref[pl.ds(rows, 256), 0:BLK] = xb[slot, :, pl.ds(mine, 256)].T
+
+        @pl.when(b < 6)
+        def _():
+            load_x(b + 2).start()
+
+    def take_x(b):
+        x_copy(b).wait_recv()
+        rows = pl.multiple_of(b * 256, 256)
+        xt_ref[pl.ds(rows, 256), BLK : 2 * BLK] = xr[b].astype(BF16).T
+
+    LAG = 3
+    BEHIND = 2
+
+    def slot_step(i, carry):
+        def step(st, delay, body):
+            j = i - LAG * (z if st else 3 - z) - (BEHIND if st else 0) - delay
+
+            @pl.when(jnp.logical_and(j >= 0, j < 8))
+            def _():
+                body(j)
+
+        def settled(j):
+            settle(0, j)
+            finish_v(core * 8 + j)
+
+        def received(j):
+            receive(0, j)
+            finish_v((1 - core) * 8 + j)
+
+        step(0, 0, lambda j: chain(0, j))
+        step(0, LAG, settled)
+        step(0, LAG + 1, received)
+
+        @pl.when(i < 8)
+        def _():
+            sum_keys(i)
+
+        step(1, 0, lambda j: chain(1, j))
+        step(1, LAG, lambda j: settle(1, j))
+
+        @pl.when(i < 8)
+        def _():
+            send_x(i)
+            local(core * 8 + i)
+            local((1 - core) * 8 + i)
+
+        @pl.when(jnp.logical_and(i >= 8, i < 16))
+        def _():
+            take_x(i - 8)
+
+        return carry
+
+    lax.fori_loop(0, 8 + 4 * LAG + BEHIND, slot_step, 0)
+
+    def each(count, body):
+        def run(i, carry):
+            body(i)
+            return carry
+
+        lax.fori_loop(0, count, run, 0)
+
+    store = pltpu.make_async_copy(kb, gv_hbm, out_sem.at[0])
+    store.start()
     each(8, lambda j: receive(1, j))
-
-    def finish_q(head):
-        total = gq[head] + nt(gb[:, lanes(head)], state[1, head])
-        gb[:, lanes(head)] = total.astype(BF16)
-
-    each(16, finish_q)
-    stores[0].start()
 
     def take_d(head):
         d_copy(head).wait_recv()
@@ -497,8 +549,7 @@
                 z_copy(st, j).wait_send()
 
         each(8, drain)
-    for store in stores:
-        store.wait()
+    store.wait()
 
 
 def grads(x, q, k, v, g):
@@ -511,23 +562,23 @@
     return pl.pallas_call(
         grads_kernel,
         out_shape=(
-            wide, wide, wide,
+            wide,
             jax.ShapeDtypeStruct((2048, 1024), BF16),
             jax.ShapeDtypeStruct((2, 1024, 1024), BF16),
+            jax.ShapeDtypeStruct((2, H, HDIM, HDIM), BF16),
         ),
         in_specs=[any_spec] * 5,
-        out_specs=(any_spec,) * 3 + (vmem_spec,) * 2,
+        out_specs=(any_spec,) + (vmem_spec,) * 3,
         scratch_shapes=[
             *[pltpu.VMEM((BLK, HD), BF16)] * 4,
             pltpu.VMEM((2, 2, 8, HDIM, HDIM), F32),
             *[hop] * 7,
-            pltpu.VMEM((2, H, HDIM, HDIM), BF16),
-            *[partial] * 3,
+            partial,
             pltpu.VMEM((2, BLK, 512), BF16),
             pltpu.VMEM((2, BLK, 256), F32),
             pltpu.VMEM((8, BLK, 256), F32),
             partial, partial,
-            dma((4,)), dma((2,)), dma((3,)),
+            dma((4,)), dma((2,)), dma((1,)),
             *[(dma((2, 8)), dma((2, 8)))] * 4,
             (dma((8,)), dma((8,))),
             (dma((H,)), dma((H,))),
@@ -541,8 +592,9 @@
 
 def per_device(layer_input, queries, key_vectors, value_vectors, grad_output):
     arrays = (layer_input, queries, key_vectors, value_vectors, grad_output)
-    gq, gk, gv, xt, dvh = grads(*(array[0] for array in arrays))
-    grad_weight = weight(xt, dvh)
+    x, q, k, v, g = (array[0] for array in arrays)
+    gv, xt, dvh, state = grads(x, q, k, v, g)
+    grad_weight, gq, gk = weight(xt, dvh, state, q, k, v, g)
     return (gq[None], gk[None], gv[None], grad_weight)
 
 

time: 158 us -> 147 us (0.930)
  Pallas kernels: 150 us -> 139 us
    pallas_call x2, Pallas kernels: 150 us -> 139 us  [the longest x1 92.1 us: weight(): pl.pallas_call(weight_kernel, out_shape=(jax.ShapeDtypeStruct((256, 256),...]
    unnamed x12 -> x10, local copies, waits for them, and re-layouts: 6.72 us -> 7.68 us
where the time goes in v3:
time: 147 us
  Pallas kernels  139 us (95%)
  local copies, waits for them, and re-layouts  7.68 us (5%)
    pallas_call x1, Pallas kernels, weight(): pl.pallas_call(weight_kernel, out_shape=(jax.ShapeDtypeStruct((256, 256),...  92.1 us
    pallas_call x1, Pallas kernels, grads(): pl.pallas_call(grads_kernel, out_shape=(wide, jax.ShapeDtypeStruct((2048,...  46.8 us
    unnamed x10, local copies, waits for them, and re-layouts  7.68 us

profile of v3, /device:TPU:0, one launch (start us, length us, event | category | flops | bytes accessed | tf_op | source)
XLA Modules:
  0.0 147.2 jit_solution(9876767179015086443)
XLA Ops:
  0.6 46.8 %grads.1 = (bf16[512,2048]{1,0:T(8,128)(2,1)}, bf16[2048,1024]{1,0:T(8,128)(2,1)}, bf16[2,1024,1024]{2,1,0:T(8,128)(2,1)}, bf16[2,16,128,128]{3,2,1,0:T(8,128)(2,1)}) custom-call(bf16[512,4096]{1,0:T(8,128)(2,1)} %bitcast.16, bf16[512,2048]{1,0:T(8,128)(2,1)} %bitcast.8, bf16[512,2048]{1,0:T(8,128)(2,1)} %bitcast.10, bf16[512,2048]{1,0:T(8,128)(2,1)} %bitcast.12, ...), custom_call_target="tpu_custom_call" | custom-call | tf_op jit(solution)/shard_map/grads/pallas_call | solution.py:562
  47.4 92.1 %weight_rs.1 = (f32[256,256]{1,0:T(8,128)}, bf16[512,2048]{1,0:T(8,128)(2,1)}, bf16[512,2048]{1,0:T(8,128)(2,1)}) custom-call(bf16[2048,1024]{1,0:T(8,128)(2,1)} %get-tuple-element.11.xt_ref, bf16[2,1024,1024]{2,1,0:T(8,128)(2,1)} %get-tuple-element.12.dv_ref, bf16[2,16,128,128]{3,2,1,0:T(8,128)(2,1)} %get-tuple-element.13.state_ref, ...), custom_call_target="tpu_custom_call" | custom-call | tf_op jit(solution)/shard_map/weight_rs/pallas_call | solution.py:292
  139.6 0.0 copy-start.1
  139.6 3.3 %copy.13 = bf16[1,512,2048]{2,1,0:T(8,128)(2,1)} copy(bf16[1,512,2048]{2,1,0:T(8,128)(2,1)} %bitcast.19) | data formatting | bytes 4194304
  142.9 0.0 copy-done.1
  142.9 0.0 copy-start
  142.9 1.3 copy.14
  144.2 1.0 copy-done
  145.2 0.0 copy-start.2
  145.2 1.3 copy.15
  146.5 0.0 copy-done.2
  146.5 0.7 copy.16
Async XLA Ops:
  139.6 3.3 %copy-start.1 = (bf16[512,2048]{1,0:T(8,128)(2,1)S(1)}, bf16[512,2048]{1,0:T(8,128)(2,1)}, u32[]{:S(2)}) copy-start(bf16[512,2048]{1,0:T(8,128)(2,1)} %get-tuple-element.15) | copy-start | bytes 6291460
  142.9 2.3 %copy-start = (bf16[512,2048]{1,0:T(8,128)(2,1)S(1)}, bf16[512,2048]{1,0:T(8,128)(2,1)}, u32[]{:S(2)}) copy-start(bf16[512,2048]{1,0:T(8,128)(2,1)} %get-tuple-element.16) | copy-start | bytes 6291460
  145.2 1.3 copy-start.2

commit v4 on v1

v4 whole, which is shorter than its diff:
```python
import jax
import jax.numpy as jnp
from jax import lax
from jax.experimental import pallas as pl
from jax.experimental.pallas import tpu as pltpu
from jax.sharding import PartitionSpec as P

MESH = pl.DeviceIdType.MESH
H = 16
HDIM = 128
BLK = 512
HD = 2048
F32 = jnp.float32
BF16 = jnp.bfloat16

ROWS = {
    (0, 0): (48, 40), (0, 1): (40, 48), (0, 2): (40, 40),
    (1, 0): (40, 48), (1, 1): (48, 40), (1, 2): (40, 40),
}
ORDER = (("x", "y", "z"), ("y", "z", "x"), ("z", "x", "y"))
UNITS = [(h, c, f) for h in range(2) for c in range(3) for f in range(2)]


def row_start(h, c, f):
    start = sum(sum(ROWS[(h, prior)]) for prior in range(c))
    return start + (ROWS[(h, c)][0] if f else 0)


def place():
    seq, grp = lax.axis_index("seq"), lax.axis_index("grp")
    core = lax.rem(seq, 2)
    y_lo = lax.rem(lax.div(seq, 2), 2)
    return {
        "x": lax.rem(grp, 4),
        "y": lax.div(grp, 4) * 2 + y_lo,
        "z": lax.div(seq, 4),
        "core": core,
    }


def device(at):
    return (
        at["z"] * 4 + lax.rem(at["y"], 2) * 2 + at["core"],
        lax.div(at["y"], 2) * 4 + at["x"],
    )


def shifted(at, axis, delta):
    moved = dict(at)
    moved[axis] = lax.rem(at[axis] + delta + 4, 4)
    return device(moved)


def partner_of(at):
    moved = dict(at)
    moved["core"] = 1 - at["core"]
    return device(moved)


def greet(devices):
    barrier = pltpu.get_barrier_semaphore()
    for other in devices:
        pl.semaphore_signal(barrier, inc=1, device_id=other, device_id_type=MESH)
    pl.semaphore_wait(barrier, len(devices))


def lanes(head):
    return pl.ds(pl.multiple_of(head * HDIM, HDIM), HDIM)


def nt(lhs, rhs):
    return lax.dot_general(lhs, rhs, (((1,), (1,)), ((), ())), preferred_element_type=F32)


def nn(lhs, rhs):
    return jnp.dot(lhs, rhs, preferred_element_type=F32)


HALF = BLK // 2


def lower(block):
    row = lax.broadcasted_iota(jnp.int32, (HALF, HALF), 0)
    col = lax.broadcasted_iota(jnp.int32, (HALF, HALF), 1)
    return jnp.where(col <= row, block, 0.0).astype(BF16)


def upper(block):
    row = lax.broadcasted_iota(jnp.int32, (HALF, HALF), 0)
    col = lax.broadcasted_iota(jnp.int32, (HALF, HALF), 1)
    return jnp.where(row <= col, block, 0.0).astype(BF16)


def kernel(
    x_hbm, q_hbm, k_hbm, v_hbm, g_hbm,
    gq_hbm, gk_hbm, gv_hbm, out_ref,
    qb, kb, vb, gb, xt_ref, dvh_ref, state,
    sums, paired, zgot, zsend, ygot, ysend, fgot, fsend, xb, xs, tiles,
    load_sem, xload_sem, out_sem, store_sem,
    pair_send, pair_recv, z_send, z_recv, y_send, y_recv, f_send, f_recv,
    x_send, x_recv, d_send, d_recv, *landing_refs
):
    pair_sems, z_sems, y_sems = (pair_send, pair_recv), (z_send, z_recv), (y_send, y_recv)
    f_sems, x_sems, d_sems = (f_send, f_recv), (x_send, x_recv), (d_send, d_recv)
    at = place()
    core = at["core"]
    z = at["z"]
    y_lo = lax.rem(at["y"], 2)
    other = partner_of(at)
    beside = dict(at)
    beside["y"] = at["y"] + 1 - 2 * y_lo
    beside = device(beside)

    loads = [
        pltpu.make_async_copy(src, dst, load_sem.at[i])
        for i, (src, dst) in enumerate(
            ((q_hbm, qb), (g_hbm, gb), (k_hbm, kb), (v_hbm, vb))
        )
    ]
    for load in loads:
        load.start()

    def load_x(b):
        cols = pl.multiple_of(b * 512, 512)
        slot = lax.rem(b, 2)
        return pltpu.make_async_copy(
            x_hbm.at[:, pl.ds(cols, 512)], xb.at[slot], xload_sem.at[slot]
        )

    load_x(0).start()
    load_x(1).start()

    def remote(src, dst, sems, index, target):
        send, recv = sems
        for i in index:
            send, recv = send.at[i], recv.at[i]
        return pltpu.make_async_remote_copy(
            src_ref=src, dst_ref=dst, send_sem=send, recv_sem=recv,
            device_id=target, device_id_type=MESH,
        )

    def pair_copy(st, j):
        return remote(sums.at[st, 1 - core, j], paired.at[st, j], pair_sems, (st, j), other)

    def z_copy(st, j):
        return remote(
            zsend.at[st, j], zgot.at[st, j], z_sems, (st, j),
            shifted(at, "z", 1 if st else -1),
        )

    def y_copy(st, j):
        return remote(ysend.at[st, j], ygot.at[st, j], y_sems, (st, j), beside)

    def f_copy(st, j):
        return remote(fsend.at[st, j], fgot.at[st, j], f_sems, (st, j), other)

    def x_copy(b):
        return remote(
            xs.at[lax.rem(b, 2)],
            tiles.at[lax.div(b, 4), pl.ds(48 + lax.rem(b, 4) * 4, 4)],
            x_sems, (b,), other,
        )

    def d_copy(head):
        h, place_in = lax.rem(head, 2), lax.div(head, 2)
        return remote(
            tiles.at[h, pl.ds(16 + 2 * place_in, 2)],
            tiles.at[h, pl.ds(32 + 2 * place_in, 2)],
            d_sems, (head,), other,
        )

    def v_store(head):
        h, place_in = lax.rem(head, 2), lax.div(head, 2)
        return pltpu.make_async_copy(
            dvh_ref.at[h, 0:BLK, lanes(place_in)], gv_hbm.at[:, lanes(head)], out_sem.at[head]
        )

    def head_of(which, j):
        return which * 8 + lax.rem(j, 4) * 2 + lax.div(j, 4)

    for st in range(2):
        @pl.when(z == (0 if st else 3))
        def _(st=st):
            zgot[st] = jnp.zeros((8, HDIM, HDIM), F32)

    greet([other] + [shifted(at, axis, delta) for axis in "xyz" for delta in (1, -1)])

    def outer(lhs, rhs, head):
        return lax.dot_general(
            lhs[:, lanes(head)], rhs[:, lanes(head)], (((0,), (0,)), ((), ())),
            preferred_element_type=F32,
        )

    loads[0].wait()
    loads[1].wait()

    def theirs(j, carry):
        sums[0, 1 - core, j] = outer(qb, gb, head_of(1 - core, j))
        pair_copy(0, j).start()
        return carry

    def mine(j, carry):
        sums[0, core, j] = outer(qb, gb, head_of(core, j))
        return carry

    lax.fori_loop(0, 8, theirs, 0)
    lax.fori_loop(0, 8, mine, 0)
    loads[2].wait()
    loads[3].wait()

    def sum_keys(j):
        sums[1, 1 - core, j] = outer(kb, vb, head_of(1 - core, j))
        pair_copy(1, j).start()
        sums[1, core, j] = outer(kb, vb, head_of(core, j))

    def chain(st, j):
        pair_copy(st, j).wait_recv()

        @pl.when(z != (0 if st else 3))
        def _():
            z_copy(st, j).wait_recv()

        chip = sums[st, core, j] + paired[st, j]
        far = zgot[st, j]
        zsend[st, j] = chip + far
        full = y_lo == (0 if st else 1)
        ysend[st, j] = far + jnp.where(full, chip, 0.0)

        @pl.when(z != (3 if st else 0))
        def _():
            z_copy(st, j).start()

        y_copy(st, j).start()

    def settle(st, j):
        y_copy(st, j).wait_recv()
        both = zgot[st, j] + ygot[st, j]
        inner = 1 if st else 0
        fsend[st, j] = both + jnp.where(core != inner, sums[st, core, j], 0.0)
        f_copy(st, j).start()
        state[st, head_of(core, j)] = (
            both + jnp.where(core == inner, paired[st, j], 0.0)
        ).astype(BF16)

    def receive(st, j):
        f_copy(st, j).wait_recv()
        state[st, head_of(1 - core, j)] = fgot[st, j].astype(BF16)

    def local(head):
        q, k, g = qb[:, lanes(head)], kb[:, lanes(head)], gb[:, lanes(head)]
        q0, q1, k0, k1 = q[:HALF], q[HALF:], k[:HALF], k[HALF:]
        g0, g1 = g[:HALF], g[HALF:]
        h, first = lax.rem(head, 2), lax.div(head, 2) * 2
        tiles[h, first] = nn(upper(nt(k0, q0)), g0) + nn(nt(k0, q1).astype(BF16), g1)
        tiles[h, first + 1] = nn(upper(nt(k1, q1)), g1)

    def finish_v(head):
        h, place_in = lax.rem(head, 2), lax.div(head, 2)
        after = state[0, head]
        for part in range(2):
            rows = slice(part * HALF, part * HALF + HALF)
            index = 2 * place_in + part
            total = tiles[h, index] + nn(kb[rows, lanes(head)], after)
            rounded = total.astype(BF16)
            tiles[h, 16 + index] = rounded.astype(F32)
            dvh_ref[h, rows, lanes(place_in)] = rounded
        d_copy(head).start()
        v_store(head).start()

    def send_x(b):
        slot = lax.rem(b, 2)
        load_x(b).wait()

        @pl.when(b >= 2)
        def _():
            x_copy(b - 2).wait_send()

        theirs = pl.multiple_of((1 - core) * 256, 256)
        mine = pl.multiple_of(core * 256, 256)
        for part in range(2):
            wide = xb[slot, part * 256 : part * 256 + 256, pl.ds(theirs, 256)].astype(F32)
            for side in range(2):
                xs[slot, 2 * part + side] = wide[:, side * 128 : side * 128 + 128]
        x_copy(b).start()
        rows = pl.multiple_of(b * 256, 256)
        xt_ref[pl.ds(rows, 256), 0:BLK] = xb[slot, :, pl.ds(mine, 256)].T

        @pl.when(b < 6)
        def _():
            load_x(b + 2).start()

    def take_x(b):
        x_copy(b).wait_recv()
        rows = pl.multiple_of(b * 256, 256)
        first = 48 + lax.rem(b, 4) * 4
        for part in range(2):
            for side in range(2):
                block = tiles[lax.div(b, 4), first + 2 * part + side].astype(BF16)
                xt_ref[
                    pl.ds(rows + side * 128, 128),
                    BLK + part * 256 : BLK + part * 256 + 256,
                ] = block.T

    LAG = 3
    BEHIND = 1

    def slot_step(i, carry):
        def step(st, delay, body):
            j = i - LAG * (z if st else 3 - z) - (BEHIND if st else 0) - delay

            @pl.when(jnp.logical_and(j >= 0, j < 8))
            def _():
                body(j)

        def settled(j):
            settle(0, j)
            finish_v(head_of(core, j))

        def received(j):
            receive(0, j)
            finish_v(head_of(1 - core, j))

        step(0, 0, lambda j: chain(0, j))
        step(0, LAG, settled)
        step(0, LAG + 1, received)

        @pl.when(i < 8)
        def _():
            sum_keys(i)

        step(1, 0, lambda j: chain(1, j))
        step(1, LAG, lambda j: settle(1, j))

        @pl.when(i < 8)
        def _():
            send_x(i)
            local(head_of(core, i))
            local(head_of(1 - core, i))

        @pl.when(jnp.logical_and(i >= 8, i < 16))
        def _():
            take_x(i - 8)

        return carry

    send_sem, recv_sem = landing_refs[3 * len(UNITS) :]
    landing = {unit: landing_refs[3 * i : 3 * i + 3] for i, unit in enumerate(UNITS)}

    def piece(unit, stage, chunk):
        h, c, f = unit
        count = 4 ** (2 - stage)
        base = chunk * count
        for earlier in range(stage):
            base = base + at[ORDER[c][earlier]] * 4 ** (2 - earlier)
        start = row_start(*unit)
        return tiles.at[h, pl.ds(base, count), start : start + ROWS[(h, c)][f]]

    def hop(unit, stage, kind):
        index = UNITS.index(unit)
        axis = ORDER[unit[1]][stage]
        sign = 1 if unit[2] else -1
        mine = at[axis]
        chunk, toward = (
            (lax.rem(mine + 2, 4), sign),
            (lax.rem(mine - sign + 4, 4), -sign),
            (lax.rem(mine + sign + 4, 4), sign),
        )[kind]
        return pltpu.make_async_remote_copy(
            src_ref=piece(unit, stage, chunk),
            dst_ref=landing[unit][stage].at[kind],
            send_sem=send_sem.at[index, stage, kind],
            recv_sem=recv_sem.at[index, stage, kind],
            device_id=shifted(at, axis, toward),
            device_id_type=MESH,
        )

    def compute(h):
        def block(b, carry):
            rows = pl.multiple_of(b * 256, 256)
            z_to, y_to = lax.div(b, 2), lax.rem(b, 2)
            lhs = xt_ref[pl.ds(rows, 256), :]
            for pair in range(4):
                acc = jnp.dot(
                    lhs,
                    dvh_ref[h, :, pair * 256 : pair * 256 + 256],
                    preferred_element_type=F32,
                )
                for side in range(2):
                    tile = 2 * pair + side
                    dest = {"x": tile % 4, "y": (tile // 4) * 2 + y_to, "z": z_to}
                    for c in range(3):
                        i, j, k = (dest[axis] for axis in ORDER[c])
                        start = row_start(h, c, 0)
                        stop = start + sum(ROWS[(h, c)])
                        tiles[h, i * 16 + j * 4 + k, start:stop] = acc[
                            start:stop, side * 128 : side * 128 + 128
                        ]
            return carry

        lax.fori_loop(0, 8, block, 0)

    def units_of(h):
        return [unit for unit in UNITS if unit[0] == h]

    def issue(h, stage):
        for kind in range(2):
            for unit in units_of(h):
                hop(unit, stage, kind).start()

    def combine(h, stage):
        for unit in units_of(h):
            axis = ORDER[unit[1]][stage]
            sign = 1 if unit[2] else -1
            hop(unit, stage, 0).wait_recv()
            target = piece(unit, stage, lax.rem(at[axis] + sign + 4, 4))
            arrived = landing[unit][stage].at[0]
            if stage == 0:
                def add(i, carry, target=target, arrived=arrived):
                    four = pl.ds(i * 4, 4)
                    target[four] = target[four] + arrived[four]
                    return carry

                lax.fori_loop(0, 4, add, 0)
            else:
                target[...] = target[...] + arrived[...]
            hop(unit, stage, 2).start()

    def final(h, stage, then):
        for unit in units_of(h):
            axis = ORDER[unit[1]][stage]
            hop(unit, stage, 1).wait_recv()
            hop(unit, stage, 2).wait_recv()
            target = piece(unit, stage, at[axis])
            direct = landing[unit][stage].at[1]
            summed = landing[unit][stage].at[2]
            if stage == 0:
                def add(i, carry, target=target, direct=direct, summed=summed):
                    four = pl.ds(i * 4, 4)
                    target[four] = target[four] + direct[four] + summed[four]
                    return carry

                lax.fori_loop(0, 4, add, 0)
            elif stage == 1:
                target[...] = target[...] + direct[...] + summed[...]
            else:
                start = row_start(*unit)
                total = target[0] + direct[0] + summed[0]
                out_ref[start : start + ROWS[unit[:2]][unit[2]], h * 128 : h * 128 + 128] = (
                    total * SCALE
                )
            if then:
                hop(unit, stage + 1, 0).start()
                hop(unit, stage + 1, 1).start()

    def attend(head):
        q, k = qb[:, lanes(head)], kb[:, lanes(head)]
        v, g = vb[:, lanes(head)], gb[:, lanes(head)]
        q0, q1, k0, k1 = q[:HALF], q[HALF:], k[:HALF], k[HALF:]
        v0, v1, g0, g1 = v[:HALF], v[HALF:], g[:HALF], g[HALF:]
        after, before = state[0, head], state[1, head]
        gk0 = nn(upper(nt(v0, g0)), q0) + nn(nt(v0, g1).astype(BF16), q1) + nt(v0, after)
        gk1 = nn(upper(nt(v1, g1)), q1) + nt(v1, after)
        gq0 = nn(lower(nt(g0, v0)), k0) + nt(g0, before)
        gq1 = (
            nn(nt(g1, v0).astype(BF16), k0) + nn(lower(nt(g1, v1)), k1) + nt(g1, before)
        )
        vb[0:HALF, lanes(head)] = gk0.astype(BF16)
        vb[HALF:BLK, lanes(head)] = gk1.astype(BF16)
        gb[0:HALF, lanes(head)] = gq0.astype(BF16)
        gb[HALF:BLK, lanes(head)] = gq1.astype(BF16)

    def fill(first, last):
        def run(head, carry):
            attend(head)
            return carry

        lax.fori_loop(first, last, run, 0)

    def each(count, body):
        def run(i, carry):
            body(i)
            return carry

        lax.fori_loop(0, count, run, 0)

    def take_d(head):
        d_copy(head).wait_recv()
        h, place_in = lax.rem(head, 2), lax.div(head, 2)
        for part in range(2):
            rows = slice(BLK + part * HALF, BLK + part * HALF + HALF)
            dvh_ref[h, rows, lanes(place_in)] = tiles[h, 32 + 2 * place_in + part].astype(BF16)
        d_copy(head).wait_send()

    SPLIT = 6 + 4 * LAG

    lax.fori_loop(0, SPLIT, slot_step, 0)
    each(2, lambda b: x_copy(b + 6).wait_send())
    each(8, lambda p: take_d(2 * p))
    compute(0)
    issue(0, 0)
    lax.fori_loop(SPLIT, 8 + 4 * LAG + BEHIND, slot_step, 0)
    each(8, lambda p: take_d(2 * p + 1))
    compute(1)
    combine(0, 0)
    issue(1, 0)
    each(8, lambda j: receive(1, j))
    fill(0, 6)
    final(0, 0, True)
    fill(6, 10)
    combine(1, 0)
    fill(10, 13)
    combine(0, 1)
    fill(13, 16)
    stores = [
        pltpu.make_async_copy(gb, gq_hbm, store_sem.at[0]),
        pltpu.make_async_copy(vb, gk_hbm, store_sem.at[1]),
    ]
    for store in stores:
        store.start()
    final(0, 1, True)
    final(1, 0, True)
    combine(0, 2)
    final(0, 2, False)
    combine(1, 1)
    final(1, 1, True)
    combine(1, 2)
    final(1, 2, False)
    for unit in UNITS:
        for stage in range(3):
            for kind in range(3):
                hop(unit, stage, kind).wait_send()
    for store in stores:
        store.wait()
    each(H, lambda head: v_store(head).wait())
    for st in range(2):
        def drain(j, st=st):
            pair_copy(st, j).wait_send()
            y_copy(st, j).wait_send()
            f_copy(st, j).wait_send()

            @pl.when(z != (3 if st else 0))
            def _():
                z_copy(st, j).wait_send()

        each(8, drain)


SCALE = 65536.0 ** -0.5


def per_device(layer_input, queries, key_vectors, value_vectors, grad_output):
    arrays = (layer_input, queries, key_vectors, value_vectors, grad_output)
    wide = jax.ShapeDtypeStruct((BLK, HD), BF16)
    dma = pltpu.SemaphoreType.DMA
    hop = pltpu.VMEM((2, 8, HDIM, HDIM), F32)
    any_spec = pl.BlockSpec(memory_space=pl.ANY)
    landing = []
    for h, c, f in UNITS:
        for count in (16, 4, 1):
            landing.append(pltpu.VMEM((3, count, ROWS[(h, c)][f], 128), F32))
    gq, gk, gv, grad_weight = pl.pallas_call(
        kernel,
        out_shape=(wide, wide, wide, jax.ShapeDtypeStruct((256, 256), F32)),
        in_specs=[any_spec] * 5,
        out_specs=(any_spec,) * 3 + (pl.BlockSpec(memory_space=pltpu.VMEM),),
        scratch_shapes=[
            *[pltpu.VMEM((BLK, HD), BF16)] * 4,
            pltpu.VMEM((2048, 1024), BF16),
            pltpu.VMEM((2, 1024, 1024), BF16),
            pltpu.VMEM((2, H, HDIM, HDIM), BF16),
            pltpu.VMEM((2, 2, 8, HDIM, HDIM), F32),
            *[hop] * 7,
            pltpu.VMEM((2, BLK, 512), BF16),
            pltpu.VMEM((2, 4, 256, 128), F32),
            pltpu.VMEM((2, 64, 256, 128), F32),
            dma((4,)), dma((2,)), dma((H,)), dma((2,)),
            *[dma((2, 8))] * 8,
            dma((8,)), dma((8,)), dma((H,)), dma((H,)),
            *landing,
            dma((len(UNITS), 3, 3)), dma((len(UNITS), 3, 3)),
        ],
        compiler_params=pltpu.CompilerParams(
            collective_id=1, has_side_effects=True, vmem_limit_bytes=63 << 20
        ),
        name="fused",
    )(*(array[0] for array in arrays))
    return (gq[None], gk[None], gv[None], grad_weight)


def solution(mesh):
    return jax.shard_map(
        per_device,
        mesh=mesh,
        in_specs=(
            P("grp", "seq", None),
            P("grp", "seq", None),
            P("grp", "seq", None),
            P("grp", "seq", None),
            P("grp", "seq", None),
        ),
        out_specs=(
            P("grp", "seq", None),
            P("grp", "seq", None),
            P("grp", "seq", None),
            P("seq", "grp"),
        ),
        check_vma=False,
    )
```

time: 349 us -> 135 us (0.39)
  waiting for transfers between devices: 69.8 us -> 0 us
  matrix products: 51.2 us -> 0 us
  other arithmetic: 48.5 us -> 0 us
  local copies, waits for them, and re-layouts: 38.1 us -> 7.68 us
  between operations: 14.3 us -> 0.65 us
    all_gather x2 -> x0, waiting for transfers between devices: 69.8 us -> none  [prefix(): pieces = lax.all_gather(value, axis)]
    dot_general x9 -> x0, matrix products: 51.2 us -> none  [the longest x1 8.79 us: per_device(): jnp.einsum('bhts,bshe->bthe', back, k_blocks, preferred_element_type=jnp....]
    select_n x30 -> x0, other arithmetic: 48.3 us -> none  [step(): return jnp.where(position < mine, longer, total)]
    unnamed x31 -> x10, local copies, waits for them, and re-layouts: 21.2 us -> 7.68 us
    rev x1 -> x0, local copies, waits for them, and re-layouts: 11.6 us -> none  [prefix(): pieces = pieces[::-1]]
    pallas_call x2 -> x1, Pallas kernels: 125 us -> 127 us  [per_device(): pl.pallas_call(kernel, out_shape=(wide, wide, wide, jax.ShapeDtypeStruct(...]
  transfers between devices with their start and end apart: 2 -> 0, of which waited for: 1 -> 0; matrix products, arithmetic and copies ran while one was open for 21% -> 0% of each run, Pallas kernels for 36% -> 0%
where the time goes in v4:
time: 135 us
  Pallas kernels  127 us (94%)
  local copies, waits for them, and re-layouts  7.68 us (6%)
    pallas_call x1, Pallas kernels, per_device(): pl.pallas_call(kernel, out_shape=(wide, wide, wide, jax.ShapeDtypeStruct(...  127 us
    unnamed x10, local copies, waits for them, and re-layouts  7.68 us

profile of v4, /device:TPU:0, one launch (start us, length us, event | category | flops | bytes accessed | tf_op | source)
XLA Modules:
  0.0 135.0 jit_solution(9502387897734609629)
XLA Ops:
  0.6 126.7 %fused.1 = (bf16[512,2048]{1,0:T(8,128)(2,1)}, bf16[512,2048]{1,0:T(8,128)(2,1)}, bf16[512,2048]{1,0:T(8,128)(2,1)}, f32[256,256]{1,0:T(8,128)}) custom-call(bf16[512,4096]{1,0:T(8,128)(2,1)} %bitcast.8, bf16[512,2048]{1,0:T(8,128)(2,1)} %bitcast.12, bf16[512,2048]{1,0:T(8,128)(2,1)} %bitcast.13, bf16[512,2048]{1,0:T(8,128)(2,1)} %bitcast.14, ...), custom_call_target="tpu_custom_call" | custom-call | tf_op jit(solution)/shard_map/fused/pallas_call | solution.py:561
  127.3 0.0 copy-start.1
  127.3 3.3 %copy.13 = bf16[1,512,2048]{2,1,0:T(8,128)(2,1)} copy(bf16[1,512,2048]{2,1,0:T(8,128)(2,1)} %bitcast.11) | data formatting | bytes 4194304
  130.6 0.0 copy-done.1
  130.6 0.0 copy-start
  130.6 1.3 copy.14
  132.0 1.0 copy-done
  133.0 0.0 copy-start.2
  133.0 1.3 copy.15
  134.3 0.0 copy-done.2
  134.3 0.7 copy.16
Async XLA Ops:
  127.3 3.3 %copy-start.1 = (bf16[512,2048]{1,0:T(8,128)(2,1)S(1)}, bf16[512,2048]{1,0:T(8,128)(2,1)}, u32[]{:S(2)}) copy-start(bf16[512,2048]{1,0:T(8,128)(2,1)} %get-tuple-element.9) | copy-start | bytes 6291460
  130.6 2.3 %copy-start = (bf16[512,2048]{1,0:T(8,128)(2,1)S(1)}, bf16[512,2048]{1,0:T(8,128)(2,1)}, u32[]{:S(2)}) copy-start(bf16[512,2048]{1,0:T(8,128)(2,1)} %get-tuple-element.10) | copy-start | bytes 6291460
  133.0 1.3 copy-start.2

commit v5 on v4

--- a/solution.py
+++ b/solution.py
@@ -517,12 +517,12 @@
     ]
     for store in stores:
         store.start()
+    final(1, 0, True)
     final(0, 1, True)
-    final(1, 0, True)
+    combine(1, 1)
     combine(0, 2)
+    final(1, 1, True)
     final(0, 2, False)
-    combine(1, 1)
-    final(1, 1, True)
     combine(1, 2)
     final(1, 2, False)
     for unit in UNITS:

time: 135 us -> 132 us (0.978)
  Pallas kernels: 127 us -> 124 us
    pallas_call x1, Pallas kernels: 127 us -> 124 us  [per_device(): pl.pallas_call(kernel, out_shape=(wide, wide, wide, jax.ShapeDtypeStruct(...]
where the time goes in v5:
time: 132 us
  Pallas kernels  124 us (94%)
  local copies, waits for them, and re-layouts  7.68 us (6%)
    pallas_call x1, Pallas kernels, per_device(): pl.pallas_call(kernel, out_shape=(wide, wide, wide, jax.ShapeDtypeStruct(...  124 us
    unnamed x10, local copies, waits for them, and re-layouts  7.68 us

profile of v5, /device:TPU:0, one launch (start us, length us, event | category | flops | bytes accessed | tf_op | source)
XLA Modules:
  0.0 131.9 jit_solution(15450927202244074315)
XLA Ops:
  0.6 123.6 %fused.1 = (bf16[512,2048]{1,0:T(8,128)(2,1)}, bf16[512,2048]{1,0:T(8,128)(2,1)}, bf16[512,2048]{1,0:T(8,128)(2,1)}, f32[256,256]{1,0:T(8,128)}) custom-call(bf16[512,4096]{1,0:T(8,128)(2,1)} %bitcast.8, bf16[512,2048]{1,0:T(8,128)(2,1)} %bitcast.12, bf16[512,2048]{1,0:T(8,128)(2,1)} %bitcast.13, bf16[512,2048]{1,0:T(8,128)(2,1)} %bitcast.14, ...), custom_call_target="tpu_custom_call" | custom-call | tf_op jit(solution)/shard_map/fused/pallas_call | solution.py:561
  124.2 0.0 copy-start.1
  124.2 3.3 %copy.13 = bf16[1,512,2048]{2,1,0:T(8,128)(2,1)} copy(bf16[1,512,2048]{2,1,0:T(8,128)(2,1)} %bitcast.11) | data formatting | bytes 4194304
  127.5 0.0 copy-done.1
  127.5 0.0 copy-start
  127.5 1.3 copy.14
  128.9 1.0 copy-done
  129.9 0.0 copy-start.2
  129.9 1.3 copy.15
  131.2 0.0 copy-done.2
  131.2 0.7 copy.16
Async XLA Ops:
  124.2 3.3 %copy-start.1 = (bf16[512,2048]{1,0:T(8,128)(2,1)S(1)}, bf16[512,2048]{1,0:T(8,128)(2,1)}, u32[]{:S(2)}) copy-start(bf16[512,2048]{1,0:T(8,128)(2,1)} %get-tuple-element.9) | copy-start | bytes 6291460
  127.5 2.3 %copy-start = (bf16[512,2048]{1,0:T(8,128)(2,1)S(1)}, bf16[512,2048]{1,0:T(8,128)(2,1)}, u32[]{:S(2)}) copy-start(bf16[512,2048]{1,0:T(8,128)(2,1)} %get-tuple-element.10) | copy-start | bytes 6291460
  129.9 1.3 %copy-start.2 = (f32[256,256]{1,0:T(8,128)S(1)}, f32[256,256]{1,0:T(8,128)}, u32[]{:S(2)}) copy-start(f32[256,256]{1,0:T(8,128)} %get-tuple-element.19) | copy-start | bytes 786436
